TPU v7x, 512 devices: a whole 4x4x16 slice. The times are simulated.
512 devices in a mesh: rows: 64 (over z, y_hi, core), chan: 8 (over x, y_lo).
Axes of the slice: x: 4, y: 4 (y_hi: 2, y_lo: 2; y = y_hi * 2 + y_lo), z: 16, core: 2. Of those that a mesh axis runs over, the one named last changes fastest.
Arguments:
- features: bfloat16 [256, 128, 2048], P('rows', None, 'chan'), may hold values from 0 to 12, as said below
- low_features: bfloat16 [1024, 512, 256], P('rows', 'chan'), may hold values from -6 to 6
- w_one: bfloat16 [2048, 256], P('chan'), may hold values from -0.125 to 0.125
- w_rate: bfloat16 [3, 9, 2048, 256], P(None, None, 'chan', 'rows'), may hold values from -0.046875 to 0.046875
- w_pool: bfloat16 [2048, 256], P('chan'), may hold values from -0.125 to 0.125
- b_branch: float32 [5, 256], replicated, may hold values from -3 to 3
- w_proj: bfloat16 [1280, 256], replicated, may hold values from -0.15625 to 0.15625
- b_proj: float32 [256], replicated, may hold values from -3 to 3
- w_low: bfloat16 [256, 48], replicated, may hold values from -0.375 to 0.375
- b_low: float32 [48], replicated, may hold values from -3 to 3
- w_dec_up: bfloat16 [9, 256, 256], replicated, may hold values from -0.109375 to 0.109375
- w_dec_low: bfloat16 [9, 48, 256], replicated, may hold values from -0.109375 to 0.109375
- b_dec: float32 [256], replicated, may hold values from -3 to 3
Outputs:
- context: bfloat16 [256, 128, 256], P('rows', 'chan')
- decoded: bfloat16 [1024, 512, 256], P('rows', 'chan')
Inputs may be any that keep to these rules, and one draw needn't show every extreme that they name: features are nonnegative.
All inputs are finite; a program needn't handle non-finite values.
Results may differ from a plain program's by a relative error of at most 0.019.
Values may be sent and summed in bfloat16 or wider, within the bound.
No kernel may reach another device: no remote copies, remote signals or barrier semaphores. Data moves between devices by JAX's collectives and lax.ppermute only.
A program may use at most 128 MiB of HBM per device.

v0:
```python
import jax
import jax.numpy as jnp
from jax import lax
from jax.sharding import PartitionSpec as P

RATE = 6


BLEND = (0.875, 0.625, 0.375, 0.125)


def passed_along(block, axis, distance):
    devices = range(lax.axis_size(axis))
    route = [(i - distance, i) for i in devices if i - distance in devices]
    return lax.ppermute(block, axis, route)


def padded_2(array, sides, width):
    for axis, dim in sides:
        devices, length = (lax.axis_size(axis), array.shape[dim])
        up = [(i, (i + 1) % devices) for i in range(devices - 1)]
        down = [(j, i) for i, j in up]
        last = lax.slice_in_dim(array, length - width, length, axis=dim)
        first = lax.slice_in_dim(array, 0, width, axis=dim)
        before = lax.ppermute(last, axis, up)
        after = lax.ppermute(first, axis, down)
        array = jnp.concatenate([before, array, after], axis=dim)
    return array


def move_cols(field, across):
    extent = field.shape[1]
    amount = abs(across)
    padded = jnp.pad(field, ((0, 0), (amount, amount), (0, 0)))
    return padded[:, amount + across : amount + across + extent]


def fetch_rows(features, offset):
    hop_count, remain = divmod(offset, features.shape[0])
    upper_part = features[remain:]
    upper_part = passed_along(upper_part, "rows", -hop_count)
    if remain == 0:
        return upper_part
    lower_part = features[:remain]
    lower_part = passed_along(lower_part, "rows", -hop_count - 1)
    return jnp.concatenate([upper_part, lower_part], axis=0)


def rate_matrix(features, spacing):
    sources = (fetch_rows(features, -spacing), features, fetch_rows(features, spacing))
    pieces = [
        move_cols(source, (col_step - 1) * spacing) for source in sources for col_step in range(3)
    ]
    stacked = jnp.concatenate(pieces, axis=2)
    return stacked.reshape(-1, stacked.shape[2])


def blend_axis(field, axis_pos):
    count_in = field.shape[axis_pos]
    lower_half = lax.slice_in_dim(field, 0, count_in - 1, axis=axis_pos)
    upper_half = lax.slice_in_dim(field, 1, count_in, axis=axis_pos)
    blended = jnp.stack(
        [factor * lower_half + (1.0 - factor) * upper_half for factor in BLEND], axis=axis_pos + 1
    )
    target = list(lower_half.shape)
    target[axis_pos] = 4 * (count_in - 1)
    return blended.reshape(target)


def edge_copy(padded, rows_index, rows_count, chan_index, chan_count):
    top_row = jnp.where(rows_index == 0, padded[1:2], padded[0:1])
    bottom_row = jnp.where(rows_index == rows_count - 1, padded[-2:-1], padded[-1:])
    padded = jnp.concatenate([top_row, padded[1:-1], bottom_row], axis=0)
    left_col = jnp.where(chan_index == 0, padded[:, 1:2], padded[:, 0:1])
    right_col = jnp.where(chan_index == chan_count - 1, padded[:, -2:-1], padded[:, -1:])
    return jnp.concatenate([left_col, padded[:, 1:-1], right_col], axis=1)


def tap_matrix(padded, out_rows, out_cols):
    pieces = [
        padded[row_step : row_step + out_rows, col_step : col_step + out_cols]
        for row_step in range(3)
        for col_step in range(3)
    ]
    stacked = jnp.concatenate(pieces, axis=2)
    return stacked.reshape(out_rows * out_cols, -1)


def on_device(
    features,
    low_features,
    w_one,
    w_rate,
    w_pool,
    b_branch,
    w_proj,
    b_proj,
    w_low,
    b_low,
    w_dec_up,
    w_dec_low,
    b_dec,
):
    strip_rows, map_cols, group_in = features.shape
    branch_width = w_one.shape[1]
    pixel_count = strip_rows * map_cols
    rows_index = lax.axis_index("rows")
    rows_count = lax.axis_size("rows")
    chan_index = lax.axis_index("chan")
    chan_count = lax.axis_size("chan")
    local_sum = jnp.sum(features, axis=(0, 1), dtype=jnp.float32)
    map_total = strip_rows * rows_count * map_cols
    pool_weight = w_pool.astype(jnp.float32)
    pooled = lax.psum(local_sum, "rows") / map_total
    local_term = jnp.dot(pooled, pool_weight, precision=lax.Precision.HIGHEST)
    pool_pre = lax.psum(local_term, "chan")
    pool_branch = jax.nn.relu(pool_pre + b_branch[4]).astype(jnp.bfloat16)
    head_weight = w_proj[: 4 * branch_width]
    pool_term = jnp.dot(
        pool_branch[None, :], w_proj[4 * branch_width :], preferred_element_type=jnp.float32
    )[0]
    rate_all = lax.all_gather(w_rate, "rows", axis=3, tiled=True)
    rate_outputs = []
    for rate_level in range(3):
        matrix = rate_matrix(features, RATE * (rate_level + 1))
        weight_flat = rate_all[rate_level].reshape(-1, rate_all.shape[3])
        rate_outputs.append(jnp.dot(matrix, weight_flat, preferred_element_type=jnp.float32))
    one_out = jnp.dot(
        features.reshape(pixel_count, group_in), w_one, preferred_element_type=jnp.float32
    )
    partial_value = jnp.concatenate([one_out] + rate_outputs, axis=1).reshape(
        strip_rows, map_cols, 4 * branch_width
    )
    conv_bias = b_branch[:4].reshape(-1)
    summed = lax.psum_scatter(
        partial_value.astype(jnp.bfloat16), "chan", scatter_dimension=2, tiled=True
    ).astype(jnp.float32)
    share_width = summed.shape[2]
    bias_share = lax.dynamic_slice_in_dim(conv_bias, chan_index * share_width, share_width)
    branches = jax.nn.relu(summed + bias_share).astype(jnp.bfloat16)
    weight_share = lax.dynamic_slice_in_dim(head_weight, chan_index * share_width, share_width, 0)
    partial_terms = jnp.dot(
        branches.reshape(-1, share_width), weight_share, preferred_element_type=jnp.float32
    )
    partial_terms = partial_terms.reshape(strip_rows, map_cols, branch_width)
    projected = lax.psum_scatter(
        partial_terms.astype(jnp.bfloat16), "chan", scatter_dimension=1, tiled=True
    ).astype(jnp.float32)
    context = jax.nn.relu(projected + pool_term + b_proj).astype(jnp.bfloat16)
    tile_rows_count = context.shape[0]
    tile_cols_count = context.shape[1]
    fine_rows, fine_cols = (low_features.shape[0], low_features.shape[1])
    low_flat = low_features.reshape(fine_rows * fine_cols, low_features.shape[2])
    low_mapped = jax.nn.relu(
        jnp.dot(low_flat, w_low, preferred_element_type=jnp.float32) + b_low
    ).astype(jnp.bfloat16)
    low_mapped = low_mapped.reshape(fine_rows, fine_cols, -1)
    coarse = padded_2(context, (("rows", 0), ("chan", 1)), 1)
    coarse = edge_copy(coarse, rows_index, rows_count, chan_index, chan_count).astype(jnp.float32)
    upsampled = blend_axis(coarse, 0)[2 : 4 * tile_rows_count + 2]
    upsampled = blend_axis(upsampled, 1)[:, 2 : 4 * tile_cols_count + 2].astype(jnp.bfloat16)
    joined = jnp.concatenate([upsampled, low_mapped], axis=2)
    padded = padded_2(joined, (("rows", 0), ("chan", 1)), 1)
    up_pad = padded[:, :, :branch_width]
    low_pad = padded[:, :, branch_width:]
    up_taps = tap_matrix(up_pad, fine_rows, fine_cols)
    low_taps = tap_matrix(low_pad, fine_rows, fine_cols)
    mixed = jnp.dot(
        up_taps, w_dec_up.reshape(-1, w_dec_up.shape[2]), preferred_element_type=jnp.float32
    )
    mixed = mixed + jnp.dot(
        low_taps, w_dec_low.reshape(-1, w_dec_low.shape[2]), preferred_element_type=jnp.float32
    )
    decoded = jax.nn.relu(mixed + b_dec).astype(jnp.bfloat16).reshape(fine_rows, fine_cols, -1)
    return (context, decoded)


def solution(mesh):
    in_specs = (
        P("rows", None, "chan"),
        P("rows", "chan", None),
        P("chan", None),
        P(None, None, "chan", "rows"),
        P("chan", None),
        P(),
        P(),
        P(),
        P(),
        P(),
        P(),
        P(),
        P(),
    )
    out_specs = (P("rows", "chan", None), P("rows", "chan", None))
    return jax.shard_map(
        on_device, mesh=mesh, in_specs=in_specs, out_specs=out_specs, check_vma=False
    )
```

profile of v0, /device:TPU:1, one launch (start us, length us, event | category | flops | bytes accessed | tf_op | source)
XLA Modules:
  0.0 444.1 jit_solution(6011039615057778575)
XLA Ops:
  8.9 4.9 %collective-permute-start.4 = (bf16[4,128,256]{2,1,0:T(8,128)(2,1)}, bf16[4,128,256]{2,1,0:T(8,128)(2,1)S(1)}, u32[]{:S(2)}, u32[]{:S(2)}) collective-permute-start(bf16[4,128,256]{2,1,0:T(8,128)(2,1)} %param.13), channel_id=1, source_target_pairs={{0,24},{8,32},{16,40},{24,48},{32,56},{40,64},{48,72},{56,80},{64,... | collective-permute-start | bytes 786440 | tf_op jit(solution)/shard_map/ppermute | solution.py:15
  14.8 4.3 collective-permute-start.1
  19.2 3.5 collective-permute-start.7
  22.7 4.8 %collective-permute-start = (bf16[2,128,256]{2,1,0:T(8,128)(2,1)S(1)}, bf16[2,128,256]{2,1,0:T(8,128)(2,1)S(1)}, u32[]{:S(2)}, u32[]{:S(2)}) collective-permute-start(bf16[2,128,256]{2,1,0:T(8,128)(2,1)S(1)} %get-tuple-element.31), channel_id=1, source_target_pairs={{0,16},{8,24},{16,32},{24,40},{32,48},{40,56},{48,64},{56,72},{64,... | collective-permute-start | bytes 393224 | tf_op jit(solution)/shard_map/ppermute | solution.py:15
  27.5 4.4 collective-permute-start.6
  41.4 5.1 %collective-permute-done.3 = bf16[2,128,256]{2,1,0:T(8,128)(2,1)S(1)} collective-permute-done((bf16[2,128,256]{2,1,0:T(8,128)(2,1)S(1)}, bf16[2,128,256]{2,1,0:T(8,128)(2,1)S(1)}, u32[]{:S(2)}, u32[]{:S(2)}) %collective-permute-start.3) | collective-permute-done | bytes 131104 | tf_op jit(solution)/shard_map/ppermute | solution.py:15
  53.8 4.5 %collective-permute-done.5 = bf16[4,128,256]{2,1,0:T(8,128)(2,1)S(1)} collective-permute-done((bf16[4,128,256]{2,1,0:T(8,128)(2,1)S(1)}, bf16[4,128,256]{2,1,0:T(8,128)(2,1)S(1)}, u32[]{:S(2)}, u32[]{:S(2)}) %collective-permute-start.5) | collective-permute-done | bytes 262176 | tf_op jit(solution)/shard_map/ppermute | solution.py:15
  62.1 108.3 %all-gather.2.cloned.1.call-done = bf16[3,9,256,256]{2,0,1,3:T(4,128)(2,1)} async-done(((bf16[3,9,256,4]{2,0,1,3:T(4,128)(2,1)}), bf16[3,9,256,256]{2,0,1,3:T(4,128)(2,1)}) %all-gather.2.cloned.1.call-update) | async-done | bytes 3538960 | tf_op jit(solution)/shard_map/all_gather | solution.py:122
  170.4 12.6 %fusion.35 = (bf16[1,9,256,256]{2,0,1,3:T(2,128)(2,1)}, bf16[1,9,256,256]{2,0,1,3:T(2,128)(2,1)}, bf16[1,9,256,256]{2,0,1,3:T(2,128)(2,1)}) fusion(bf16[3,9,256,256]{2,0,1,3:T(4,128)(2,1)} %all-gather.2.cloned.1.call-done), kind=kLoop, calls=%fused_computation.137 | loop fusion | bytes 7077888 | tf_op jit(solution)/shard_map/slice | solution.py:126
  183.0 6.1 %copy.57 = bf16[1,9,256,256]{3,2,1,0:T(8,128)(2,1)} copy(bf16[1,9,256,256]{2,0,1,3:T(2,128)(2,1)} %get-tuple-element.4) | data formatting | bytes 2359296
  189.1 5.0 %copy.56 = bf16[1,9,256,256]{3,2,1,0:T(8,128)(2,1)S(1)} copy(bf16[1,9,256,256]{2,0,1,3:T(2,128)(2,1)} %get-tuple-element.3) | data formatting | bytes 2359296
  194.1 6.1 %copy.55 = bf16[1,9,256,256]{3,2,1,0:T(8,128)(2,1)} copy(bf16[1,9,256,256]{2,0,1,3:T(2,128)(2,1)} %get-tuple-element.2) | data formatting | bytes 2359296
  200.1 2.9 convolution_convert_fusion.1
  204.4 2.5 convolution_convert_fusion.3
  209.7 128.7 %psum.14 = f32[256]{0:T(256)S(1)} all-reduce(f32[256]{0:T(256)S(1)} %convert_reduce_fusion), channel_id=1, replica_groups=mesh['rows'=64,'chan'=8] {'rows'}, use_global_device_ids=true, to_apply=%region_3.4 | all-reduce | flops 256 | bytes 2048 | tf_op jit(solution)/shard_map/psum | solution.py:114
  340.7 14.7 %psum.15 = f32[256]{0:T(256)S(1)} all-reduce(f32[256]{0:T(256)S(1)} %bitcast.102), channel_id=1, replica_groups=mesh['rows'=64,'chan'=8] {'chan'}, use_global_device_ids=true, to_apply=%region_4.5 | all-reduce | flops 256 | bytes 2048 | tf_op jit(solution)/shard_map/psum | solution.py:116
  355.5 20.5 %reduce-scatter.5.cloned.1.call-done = bf16[4,16,256]{2,1,0:T(8,128)(2,1)} async-done(((bf16[4,128,256]{2,1,0:T(8,128)(2,1)}), bf16[4,16,256]{2,1,0:T(8,128)(2,1)}) %reduce-scatter.5.cloned.1.call-update) | async-done | bytes 32784 | tf_op jit(solution)/shard_map/reduce_scatter | solution.py:146
  376.8 8.0 %collective-permute-start.11 = (bf16[1,16,256]{2,1,0:T(8,128)(2,1)S(1)}, bf16[1,16,256]{2,1,0:T(8,128)(2,1)S(1)}, u32[]{:S(2)}, u32[]{:S(2)}) collective-permute-start(bf16[1,16,256]{2,1,0:T(8,128)(2,1)S(1)} %get-tuple-element.42), channel_id=1, source_target_pairs={{8,0},{16,8},{24,16},{32,24},{40,32},{48,40},{56,48},{64,56},{72,6... | collective-permute-start | bytes 24584 | tf_op jit(solution)/shard_map/ppermute | solution.py:26
  384.9 4.2 collective-permute-start.10
  391.2 4.0 collective-permute-start.12
  400.8 6.3 %collective-permute-start.14 = (bf16[1,64,304]{2,0,1:T(2,128)(2,1)S(1)}, bf16[1,64,304]{2,0,1:T(2,128)(2,1)S(1)}, u32[]{:S(2)}, u32[]{:S(2)}) collective-permute-start(bf16[1,64,304]{2,0,1:T(2,128)(2,1)S(1)} %get-tuple-element.17), channel_id=1, source_target_pairs={{0,8},{8,16},{16,24},{24,32},{32,40},{40,48},{48,56},{56,64},{64,7... | collective-permute-start | bytes 116744 | tf_op jit(solution)/shard_map/ppermute | solution.py:25
  410.1 4.2 collective-permute-start.16
  422.2 3.6 copy.43
  432.4 3.8 fusion.41
  (192 shorter events, 56.3 us)
Async XLA Ops:
  7.2 425.1 %copy-start = (bf16[9,256,256]{2,1,0:T(8,128)(2,1)S(1)}, bf16[9,256,256]{2,1,0:T(8,128)(2,1)}, u32[]{:S(2)}) copy-start(bf16[9,256,256]{2,1,0:T(8,128)(2,1)} %param.23) | copy-start | bytes 3538948
  7.2 163.2 %all-gather.2.cloned.1.call-start = ((), (), s32[]{:S(2)}) async-start(), calls=%async_computation.2 | async-start | bytes 4792320 | tf_op jit(solution)/shard_map/all_gather | solution.py:122
  8.9 329.6 %reduce-scatter.7.cloned.1.call-start = ((), (), s32[]{:S(2)}) async-start(), calls=%async_computation.4 | async-start | bytes 1179648
  8.9 40.0 %collective-permute-start.4 = (bf16[4,128,256]{2,1,0:T(8,128)(2,1)}, bf16[4,128,256]{2,1,0:T(8,128)(2,1)S(1)}, u32[]{:S(2)}, u32[]{:S(2)}) collective-permute-start(bf16[4,128,256]{2,1,0:T(8,128)(2,1)} %param.13), channel_id=1, source_target_pairs={{0,24},{8,32},{16,40},{24,48},{32,56},{40,64},{48,72},{56,80},{64,... | collective-permute-start | bytes 786440 | tf_op jit(solution)/shard_map/ppermute | solution.py:15
  14.8 18.4 %collective-permute-start.1 = (bf16[2,128,256]{2,1,0:T(8,128)(2,1)S(1)}, bf16[2,128,256]{2,1,0:T(8,128)(2,1)S(1)}, u32[]{:S(2)}, u32[]{:S(2)}) collective-permute-start(bf16[2,128,256]{2,1,0:T(8,128)(2,1)S(1)} %get-tuple-element.32), channel_id=1, source_target_pairs={{0,8},{8,16},{16,24},{24,32},{32,40},{40,48},{48,56},{56,64},{64,7... | collective-permute-start | bytes 393224 | tf_op jit(solution)/shard_map/ppermute | solution.py:15
  19.2 18.2 %collective-permute-start.7 = (bf16[2,128,256]{2,1,0:T(8,128)(2,1)S(1)}, bf16[2,128,256]{2,1,0:T(8,128)(2,1)S(1)}, u32[]{:S(2)}, u32[]{:S(2)}) collective-permute-start(bf16[2,128,256]{2,1,0:T(8,128)(2,1)S(1)} %get-tuple-element.32), channel_id=1, source_target_pairs={{0,32},{8,40},{16,48},{24,56},{32,64},{40,72},{48,80},{56,88},{64,... | collective-permute-start | bytes 393224 | tf_op jit(solution)/shard_map/ppermute | solution.py:15
  22.7 11.8 %collective-permute-start = (bf16[2,128,256]{2,1,0:T(8,128)(2,1)S(1)}, bf16[2,128,256]{2,1,0:T(8,128)(2,1)S(1)}, u32[]{:S(2)}, u32[]{:S(2)}) collective-permute-start(bf16[2,128,256]{2,1,0:T(8,128)(2,1)S(1)} %get-tuple-element.31), channel_id=1, source_target_pairs={{0,16},{8,24},{16,32},{24,40},{32,48},{40,56},{48,64},{56,72},{64,... | collective-permute-start | bytes 393224 | tf_op jit(solution)/shard_map/ppermute | solution.py:15
  27.5 11.1 %collective-permute-start.6 = (bf16[2,128,256]{2,1,0:T(8,128)(2,1)S(1)}, bf16[2,128,256]{2,1,0:T(8,128)(2,1)S(1)}, u32[]{:S(2)}, u32[]{:S(2)}) collective-permute-start(bf16[2,128,256]{2,1,0:T(8,128)(2,1)S(1)} %get-tuple-element.31), channel_id=1, source_target_pairs={{0,40},{8,48},{16,56},{24,64},{32,72},{40,80},{48,88},{56,96},{64,... | collective-permute-start | bytes 393224 | tf_op jit(solution)/shard_map/ppermute | solution.py:15
  33.2 14.7 %collective-permute-start.9 = (bf16[2,128,256]{2,1,0:T(8,128)(2,1)S(1)}, bf16[2,128,256]{2,1,0:T(8,128)(2,1)S(1)}, u32[]{:S(2)}, u32[]{:S(2)}) collective-permute-start(bf16[2,128,256]{2,1,0:T(8,128)(2,1)S(1)} %get-tuple-element.32), channel_id=1, source_target_pairs={{40,0},{48,8},{56,16},{64,24},{72,32},{80,40},{88,48},{96,56},{104... | collective-permute-start | bytes 393224 | tf_op jit(solution)/shard_map/ppermute | solution.py:15
  34.6 13.4 %collective-permute-start.8 = (bf16[2,128,256]{2,1,0:T(8,128)(2,1)S(1)}, bf16[2,128,256]{2,1,0:T(8,128)(2,1)S(1)}, u32[]{:S(2)}, u32[]{:S(2)}) collective-permute-start(bf16[2,128,256]{2,1,0:T(8,128)(2,1)S(1)} %get-tuple-element.31), channel_id=1, source_target_pairs={{32,0},{40,8},{48,16},{56,24},{64,32},{72,40},{80,48},{88,56},{96,... | collective-permute-start | bytes 393224 | tf_op jit(solution)/shard_map/ppermute | solution.py:15
  37.4 9.1 %collective-permute-start.3 = (bf16[2,128,256]{2,1,0:T(8,128)(2,1)S(1)}, bf16[2,128,256]{2,1,0:T(8,128)(2,1)S(1)}, u32[]{:S(2)}, u32[]{:S(2)}) collective-permute-start(bf16[2,128,256]{2,1,0:T(8,128)(2,1)S(1)} %get-tuple-element.32), channel_id=1, source_target_pairs={{16,0},{24,8},{32,16},{40,24},{48,32},{56,40},{64,48},{72,56},{80,... | collective-permute-start | bytes 393224 | tf_op jit(solution)/shard_map/ppermute | solution.py:15
  38.7 9.1 %collective-permute-start.2 = (bf16[2,128,256]{2,1,0:T(8,128)(2,1)S(1)}, bf16[2,128,256]{2,1,0:T(8,128)(2,1)S(1)}, u32[]{:S(2)}, u32[]{:S(2)}) collective-permute-start(bf16[2,128,256]{2,1,0:T(8,128)(2,1)S(1)} %get-tuple-element.31), channel_id=1, source_target_pairs={{8,0},{16,8},{24,16},{32,24},{40,32},{48,40},{56,48},{64,56},{72,6... | collective-permute-start | bytes 393224 | tf_op jit(solution)/shard_map/ppermute | solution.py:15
  46.5 11.7 %collective-permute-start.5 = (bf16[4,128,256]{2,1,0:T(8,128)(2,1)S(1)}, bf16[4,128,256]{2,1,0:T(8,128)(2,1)S(1)}, u32[]{:S(2)}, u32[]{:S(2)}) collective-permute-start(bf16[4,128,256]{2,1,0:T(8,128)(2,1)S(1)} %copy-done.1), channel_id=1, source_target_pairs={{24,0},{32,8},{40,16},{48,24},{56,32},{64,40},{72,48},{80,56},{88,... | collective-permute-start | bytes 786440 | tf_op jit(solution)/shard_map/ppermute | solution.py:15
  209.5 185.7 %copy-start.16 = (bf16[256,48]{0,1:T(8,128)(2,1)S(1)}, bf16[256,48]{0,1:T(8,128)(2,1)}, u32[]{:S(2)}) copy-start(bf16[256,48]{0,1:T(8,128)(2,1)} %param.21) | copy-start | bytes 73732
  209.5 185.7 %copy-start.20 = (f32[48]{0:T(128)S(1)}, f32[48]{0:T(128)}, u32[]{:S(2)}) copy-start(f32[48]{0:T(128)} %param.22) | copy-start | bytes 580
  209.5 166.5 %reduce-scatter.5.cloned.1.call-start = ((), (), s32[]{:S(2)}) async-start(), calls=%async_computation.3 | async-start | bytes 294912 | tf_op jit(solution)/shard_map/reduce_scatter | solution.py:146
  376.8 12.3 %collective-permute-start.11 = (bf16[1,16,256]{2,1,0:T(8,128)(2,1)S(1)}, bf16[1,16,256]{2,1,0:T(8,128)(2,1)S(1)}, u32[]{:S(2)}, u32[]{:S(2)}) collective-permute-start(bf16[1,16,256]{2,1,0:T(8,128)(2,1)S(1)} %get-tuple-element.42), channel_id=1, source_target_pairs={{8,0},{16,8},{24,16},{32,24},{40,32},{48,40},{56,48},{64,56},{72,6... | collective-permute-start | bytes 24584 | tf_op jit(solution)/shard_map/ppermute | solution.py:26
  384.9 5.0 %collective-permute-start.10 = (bf16[1,16,256]{2,1,0:T(8,128)(2,1)S(1)}, bf16[1,16,256]{2,1,0:T(8,128)(2,1)S(1)}, u32[]{:S(2)}, u32[]{:S(2)}) collective-permute-start(bf16[1,16,256]{2,1,0:T(8,128)(2,1)S(1)} %get-tuple-element.41), channel_id=1, source_target_pairs={{0,8},{8,16},{16,24},{24,32},{32,40},{40,48},{48,56},{56,64},{64,7... | collective-permute-start | bytes 24584 | tf_op jit(solution)/shard_map/ppermute | solution.py:25
  389.9 7.8 %collective-permute-start.13 = (bf16[6,1,256]{2,1,0:T(2,128)(2,1)S(1)}, bf16[6,1,256]{2,1,0:T(2,128)(2,1)S(1)}, u32[]{:S(2)}, u32[]{:S(2)}) collective-permute-start(bf16[6,1,256]{2,1,0:T(2,128)(2,1)S(1)} %get-tuple-element.40), channel_id=1, source_target_pairs={{1,0},{2,1},{3,2},{4,3},{5,4},{6,5},{7,6},{9,8},{10,9},{11,10},{12... | collective-permute-start | bytes 9224 | tf_op jit(solution)/shard_map/ppermute | solution.py:26
  391.2 6.5 %collective-permute-start.12 = (bf16[6,1,256]{2,1,0:T(2,128)(2,1)S(1)}, bf16[6,1,256]{2,1,0:T(2,128)(2,1)S(1)}, u32[]{:S(2)}, u32[]{:S(2)}) collective-permute-start(bf16[6,1,256]{2,1,0:T(2,128)(2,1)S(1)} %get-tuple-element.39), channel_id=1, source_target_pairs={{0,1},{1,2},{2,3},{3,4},{4,5},{5,6},{6,7},{8,9},{9,10},{10,11},{11... | collective-permute-start | bytes 9224 | tf_op jit(solution)/shard_map/ppermute | solution.py:25
  398.8 8.6 %collective-permute-start.15 = (bf16[1,64,304]{2,0,1:T(2,128)(2,1)S(1)}, bf16[1,64,304]{2,0,1:T(2,128)(2,1)S(1)}, u32[]{:S(2)}, u32[]{:S(2)}) collective-permute-start(bf16[1,64,304]{2,0,1:T(2,128)(2,1)S(1)} %get-tuple-element.18), channel_id=1, source_target_pairs={{8,0},{16,8},{24,16},{32,24},{40,32},{48,40},{56,48},{64,56},{72,6... | collective-permute-start | bytes 116744 | tf_op jit(solution)/shard_map/ppermute | solution.py:26
  400.8 8.0 %collective-permute-start.14 = (bf16[1,64,304]{2,0,1:T(2,128)(2,1)S(1)}, bf16[1,64,304]{2,0,1:T(2,128)(2,1)S(1)}, u32[]{:S(2)}, u32[]{:S(2)}) collective-permute-start(bf16[1,64,304]{2,0,1:T(2,128)(2,1)S(1)} %get-tuple-element.17), channel_id=1, source_target_pairs={{0,8},{8,16},{16,24},{24,32},{32,40},{40,48},{48,56},{56,64},{64,7... | collective-permute-start | bytes 116744 | tf_op jit(solution)/shard_map/ppermute | solution.py:25
  408.8 8.1 %collective-permute-start.17 = (bf16[18,1,304]{2,0,1:T(8,128)(2,1)S(1)}, bf16[18,1,304]{2,0,1:T(8,128)(2,1)S(1)}, u32[]{:S(2)}, u32[]{:S(2)}) collective-permute-start(bf16[18,1,304]{2,0,1:T(8,128)(2,1)S(1)} %get-tuple-element.13), channel_id=1, source_target_pairs={{1,0},{2,1},{3,2},{4,3},{5,4},{6,5},{7,6},{9,8},{10,9},{11,10},{12... | collective-permute-start | bytes 32840 | tf_op jit(solution)/shard_map/ppermute | solution.py:26
  410.1 6.8 %collective-permute-start.16 = (bf16[18,1,304]{2,0,1:T(8,128)(2,1)S(1)}, bf16[18,1,304]{2,0,1:T(8,128)(2,1)S(1)}, u32[]{:S(2)}, u32[]{:S(2)}) collective-permute-start(bf16[18,1,304]{2,0,1:T(8,128)(2,1)S(1)} %get-tuple-element.14), channel_id=1, source_target_pairs={{0,1},{1,2},{2,3},{3,4},{4,5},{5,6},{6,7},{8,9},{9,10},{10,11},{11... | collective-permute-start | bytes 32840 | tf_op jit(solution)/shard_map/ppermute | solution.py:25
  (21 other events, 682.5 us)
Sparse Core Ops, SparseCore 0:
  11.9 158.4 all-gather.1
  209.6 36.8 reduce-scatter.6
  340.6 35.3 reduce-scatter.4
where the time goes:
time: 450 us; the launch traced here: 444 us
  blocking collectives  143 us (32%)
  waiting for transfers between devices  141 us (31%)
  local copies, waits for them, and re-layouts  64.6 us (14%)
  starting transfers between devices  60.4 us (13%)
  matrix products  15.1 us (3%)
  between operations  14.8 us (3%)
  other arithmetic  4.84 us (1%)
    psum x1, blocking collectives, on_device(): pooled = lax.psum(local_sum, 'rows') / map_total  129 us
    all_gather x1, waiting for transfers between devices, on_device(): rate_all = lax.all_gather(w_rate, 'rows', axis=3, tiled=True)  108 us
    unnamed x92, local copies, waits for them, and re-layouts  37.6 us
    ppermute x10, starting transfers between devices, passed_along(): return lax.ppermute(block, axis, route)  29.1 us
    reduce_scatter x1, waiting for transfers between devices, on_device(): lax.psum_scatter(partial_terms.astype(jnp.bfloat16), 'chan', scatter_dime...  20.5 us
    ppermute x4, starting transfers between devices, padded_2(): before = lax.ppermute(last, axis, up)  18.6 us
    psum x1, blocking collectives, on_device(): pool_pre = lax.psum(local_term, 'chan')  14.7 us
    slice x1, local copies, waits for them, and re-layouts, on_device(): weight_flat = rate_all[rate_level].reshape(-1, rate_all.shape[3])  12.6 us
  transfers between devices with their start and end apart: 21, of which 7 were waited for; matrix products, arithmetic and copies ran while one was open for 4% of the time, Pallas kernels for 0%

commit v1 on v0

v1 whole, which is shorter than its diff:
```python
import functools

import jax
import jax.numpy as jnp
import numpy as np
from jax import lax
from jax.experimental import pallas as pl
from jax.experimental.pallas import tpu as pltpu
from jax.sharding import Mesh
from jax.sharding import PartitionSpec as P

RATE = 6
BLEND = (0.875, 0.625, 0.375, 0.125)
SPLIT = (("z", 16), ("yh", 2), ("core", 2), ("x", 4), ("yl", 2))
ROWS = ("z", "yh", "core")
CHAN = ("x", "yl")
BLOCK = ("x", "yl", "yh", "core")
BF = jnp.bfloat16
F32 = jnp.float32
STRIP = 4
EXT = 18
REACH = 19
UNIT = 120
PIECE = 112


def swap(axis):
    return [(0, 1), (1, 0)]


def shift_pairs(size, distance):
    return [(i, i + distance) for i in range(size) if 0 <= i + distance < size]


def halves(value):
    high = lax.reduce_precision(value, 8, 7)
    rest = value - high
    mid = lax.reduce_precision(rest, 8, 7)
    return high, mid, rest - mid


def dot_t(a, b):
    return lax.dot_general(a, b, (((1,), (1,)), ((), ())), preferred_element_type=F32)


def dot(a, b):
    return jnp.dot(a, b, preferred_element_type=F32)


def conv_kernel(
    place, eight, other, above, below, far, traded, packed, w_one, w_pool, out,
    x, rhs, wide, piece, sems,
):
    core = place[0]
    member = place[1]
    copies = []

    def fetch(source, first, count, target):
        index = len(copies)
        copy = pltpu.make_async_copy(
            source.at[pl.ds(first, count)], x.at[pl.ds(target, count)], sems.at[index]
        )
        copy.start()
        copies.append(copy)

    for half in range(2):
        mine = 8 * half + STRIP * core
        theirs = 8 * half + STRIP * (1 - core)
        fetch(eight, STRIP * half, STRIP, REACH + mine)
        fetch(other, STRIP * half, STRIP, REACH + theirs)
        fetch(above, STRIP * half, STRIP, REACH - 16 + mine)
        fetch(below, STRIP * half, STRIP, REACH + 16 + mine)
        fetch(traded, STRIP * half, STRIP, REACH - 16 + theirs)
        fetch(traded, 8 + STRIP * half, STRIP, REACH + 16 + theirs)
    fetch(far, 0, 3, 51 * (1 - core))
    fetch(traded, 16, 3, 51 * core)

    slot = (lax.broadcasted_iota(jnp.int32, (256, 256), 0) // 4) % 4
    for level in range(3):
        for index, (first, low, high) in enumerate(
            ((4 * level, 0, 2), (12 + 6 * level, 0, 2), (14 + 6 * level, 1, 3))
        ):
            rows = packed[:, 4 * first : 4 * first + 16, :].reshape(256, 256).astype(F32)
            keep = (slot >= low) & (slot <= high)
            rhs[3 * level + index] = jnp.where(keep, rows, 0.0).astype(BF)

    sums = jnp.sum(packed[:, 24:32, :].astype(F32), axis=0)
    pooled = (sums[4:5] + sums[5:6] + sums[6:7]) / float(256 * 128)
    pre = jnp.dot(
        jnp.broadcast_to(pooled, (8, 256)),
        w_pool[...].astype(F32),
        precision=lax.Precision.HIGHEST,
        preferred_element_type=F32,
    )[0:1]
    high = pre.astype(BF).astype(F32)
    mid = (pre - high).astype(BF).astype(F32)
    low = pre - high - mid
    piece[108:112, :] = jnp.concatenate([high, mid, low, jnp.zeros_like(low)], axis=0)

    wide[:, 0:8, :] = jnp.zeros((EXT, 8, 256), F32)
    wide[:, 136:144, :] = jnp.zeros((EXT, 8, 256), F32)

    for copy in copies:
        copy.wait()

    row_in = lax.broadcasted_iota(jnp.int32, (256, 256), 0)
    col_out = lax.broadcasted_iota(jnp.int32, (256, 256), 1)
    target = 4 * (row_in // 16) + row_in % 4
    lane_slot = (lax.broadcasted_iota(jnp.int32, (1, 128, 256), 2) // 4) % 4
    column = lax.broadcasted_iota(jnp.int32, (1, 128, 256), 1)
    picks = [(col_out == target + 64 * (level + 1)).astype(F32).astype(BF) for level in range(3)]
    own = (col_out == target) & ((row_in // 4) % 4 == member)
    pick_one = own.astype(F32).astype(BF)

    def chunk(step, carry):
        first = 6 * step
        centre = x[pl.ds(first + 18, 6)].reshape(768, 256)
        total = dot(dot(centre, w_one[...]).astype(BF), pick_one)
        for level in range(3):
            spacing = RATE * (level + 1)
            upper = x[pl.ds(first + 18 - spacing, 6)].reshape(768, 256)
            lower = x[pl.ds(first + 18 + spacing, 6)].reshape(768, 256)
            value = dot_t(centre, rhs[3 * level])
            value += dot_t(upper, rhs[3 * level + 1])
            value += dot_t(lower, rhs[3 * level + 2])
            value = value.reshape(6, 128, 256)
            from_left = ((lane_slot == 0) | (lane_slot == 3)) & (column >= spacing)
            from_right = (lane_slot == 2) & (column < 128 - spacing)
            moved = jnp.where(
                from_left,
                pltpu.roll(value, spacing, 1),
                jnp.where(
                    lane_slot == 1,
                    value,
                    jnp.where(from_right, pltpu.roll(value, 128 - spacing, 1), 0.0),
                ),
            ).reshape(768, 256)
            high = moved.astype(BF)
            low = (moved - high.astype(F32)).astype(BF)
            total += dot(high, picks[level]) + dot(low, picks[level])
        wide[pl.ds(first, 6), 8:136, :] = total.reshape(6, 128, 256)
        return carry

    lax.fori_loop(0, 3, chunk, 0)

    def send(part, carry):
        for tile in range(8):
            for line in range(6):
                piece[18 * line : 18 * line + 18, :] = wide[
                    STRIP * part + line, 16 * tile + 7 : 16 * tile + 25, :
                ]
            out[4 * tile + part] = piece[...].astype(BF)
        return carry

    lax.fori_loop(0, 4, send, 0)


def tail_kernel(
    received, w_proj, w_head, b_branch, b_pool, b_proj, blend, low, w_up, w_low, b_dec,
    context, decoded, cells, coarse, fine,
):
    pool = jnp.zeros((4, 256), F32)
    total = jnp.zeros((PIECE, 256), F32)
    for part in range(4):
        summed = received[part].astype(F32)
        for tile in range(1, 8):
            summed += received[4 * tile + part].astype(F32)
        pool += summed[108:112]
        branches = jnp.maximum(summed + b_branch[part : part + 1, :], 0.0).astype(BF)
        total += dot(branches, w_proj[part])
    pre = pool[0:1] + pool[1:2] + pool[2:3]
    pool_branch = jnp.maximum(pre + b_pool[...], 0.0)
    pool_term = dot(jnp.broadcast_to(pool_branch, (8, 256)).astype(BF), w_head[...])[0:1]
    value = jnp.maximum(total + pool_term + b_proj[...], 0.0)
    row = lax.broadcasted_iota(jnp.int32, (PIECE, 256), 0)
    value = jnp.where(row < 108, value, 0.0)
    cells[...] = value
    coarse[0:PIECE, :] = value.astype(BF)
    coarse[PIECE:128, :] = jnp.zeros((16, 256), BF)
    for line in range(4):
        context[line] = cells[18 * line + 19 : 18 * line + 35, :].astype(BF)
    for across in range(3):
        fine[across] = dot(blend[across], coarse[...]).astype(BF).reshape(EXT, 64, 256)
    for first in (0, 8):
        mixed = jnp.broadcast_to(b_dec[...], (512, 256))
        for down in range(3):
            mixed += dot(low[first + down : first + down + 8].reshape(512, 144), w_low[down])
            for across in range(3):
                up = fine[across, first + down : first + down + 8].reshape(512, 256)
                mixed += dot(up, w_up[3 * down + across])
        decoded[first : first + 8] = jnp.maximum(mixed, 0.0).astype(BF).reshape(8, 64, 256)


def blend_weights(count, fine_count, first, at_start, at_end):
    table = np.zeros((fine_count, count + 2), np.float32)
    for place in range(fine_count):
        index = place + first
        if (at_start and index < 2) or (at_end and index >= 4 * count + 2):
            continue
        pair, kind = divmod(index, 4)
        for cell, weight in ((pair, BLEND[kind]), (pair + 1, 1.0 - BLEND[kind])):
            cell = max(cell, 1) if at_start else cell
            cell = min(cell, count) if at_end else cell
            table[place, cell] += weight
    return table


def blend_matrix(row_index, row_count, tile_index, tile_count):
    cell = np.arange(128)
    valid = cell < 108

    def chosen(index, count, build):
        start, middle, end = build(True, False), build(False, False), build(False, True)
        value = jnp.where(index == 0, jnp.asarray(start), jnp.asarray(middle))
        return jnp.where(index == count - 1, jnp.asarray(end), value)

    def spread(table, source):
        return (table[:, np.where(valid, source, 0)] * valid).astype(np.float32)

    rows = chosen(
        row_index, row_count, lambda s, e: spread(blend_weights(4, EXT, 1, s, e), cell // 18)
    )
    blocks = []
    for across in range(3):
        cols = chosen(
            tile_index,
            tile_count,
            lambda s, e: spread(blend_weights(16, 64, 1 + across, s, e), cell % 18),
        )
        blocks.append((rows[:, None, :] * cols[None, :, :]).astype(BF).reshape(EXT * 64, 128))
    return jnp.stack(blocks)


def on_device(
    features,
    low_features,
    w_one,
    w_rate,
    w_pool,
    b_branch,
    w_proj,
    b_proj,
    w_low,
    b_low,
    w_dec_up,
    w_dec_low,
    b_dec,
):
    z_count = lax.axis_size("z")
    yh = lax.axis_index("yh")
    core = lax.axis_index("core")
    member = 2 * yh + core
    row_index = lax.axis_index(ROWS)
    row_count = lax.axis_size(ROWS)
    tile_index = lax.axis_index(CHAN)
    tile_count = lax.axis_size(CHAN)

    across_y = lax.ppermute(features, "yh", swap("yh"))
    across_y, w_rate, low_features = lax.optimization_barrier((across_y, w_rate, low_features))
    eight = jnp.where(
        yh == 0,
        jnp.concatenate([features, across_y], axis=0),
        jnp.concatenate([across_y, features], axis=0),
    )
    above = lax.ppermute(eight, "z", shift_pairs(z_count, 1))
    below = lax.ppermute(eight, "z", shift_pairs(z_count, -1))
    pairs = [(2 * i + 1, 2 * i + 5) for i in range(z_count - 2)]
    pairs += [(2 * i + 4, 2 * i) for i in range(z_count - 2)]
    far = lax.ppermute(jnp.where(core == 1, eight[5:8], eight[0:3]), ("z", "core"), pairs)
    other = lax.ppermute(eight, "core", swap("core"))

    low_flat = low_features.reshape(-1, low_features.shape[2])
    low_mapped = jax.nn.relu(jnp.dot(low_flat, w_low, preferred_element_type=F32) + b_low)
    low_mapped = low_mapped.astype(BF).reshape(16, 64, 48)
    left = lax.ppermute(low_mapped[:, 63:], CHAN, shift_pairs(tile_count, 1))
    right = lax.ppermute(low_mapped[:, :1], CHAN, shift_pairs(tile_count, -1))
    low_mapped = jnp.concatenate([left, low_mapped, right], axis=1)
    top = lax.ppermute(low_mapped[15:], ROWS, shift_pairs(row_count, 1))
    bottom = lax.ppermute(low_mapped[:1], ROWS, shift_pairs(row_count, -1))
    low_mapped = jnp.concatenate([top, low_mapped, bottom], axis=0)
    low_taps = jnp.concatenate([low_mapped[:, i : i + 64] for i in range(3)], axis=2)

    taps = jnp.transpose(w_rate, (0, 1, 3, 2))
    local_sum = jnp.sum(features, axis=(0, 1), dtype=F32)
    empty = jnp.zeros((1, 4, 256), BF)
    pool_rows = jnp.stack(halves(local_sum) + (jnp.zeros_like(local_sum),))[None].astype(BF)
    unit = []
    for level in range(3):
        unit += [taps[level, 3:6], pool_rows if level == 1 else empty]
    for level in range(3):
        unit += [taps[level, 0:3], taps[level, 7:9], taps[level, 6:7]]
    unit = jnp.concatenate(unit, axis=0).reshape(1, UNIT, 256)
    packed = lax.all_gather(unit, "z", axis=0, tiled=True)

    traded = lax.ppermute(jnp.concatenate([above, below, far], axis=0), "core", swap("core"))

    place = jnp.stack([core, member]).astype(jnp.int32)
    anywhere = pl.BlockSpec(memory_space=pl.ANY)
    on_chip = pl.BlockSpec(memory_space=pltpu.VMEM)
    pieces = pl.pallas_call(
        conv_kernel,
        name="branches",
        out_shape=jax.ShapeDtypeStruct((32, PIECE, 256), BF),
        in_specs=[pl.BlockSpec(memory_space=pltpu.SMEM)] + [anywhere] * 6 + [on_chip] * 3,
        out_specs=on_chip,
        scratch_shapes=[
            pltpu.VMEM((54, 128, 256), BF),
            pltpu.VMEM((9, 256, 256), BF),
            pltpu.VMEM((EXT, 144, 256), F32),
            pltpu.VMEM((PIECE, 256), F32),
            pltpu.SemaphoreType.DMA((14,)),
        ],
    )(place, eight, other, above, below, far, traded, packed, w_one, w_pool)
    received = lax.all_to_all(pieces, BLOCK, 0, 0, tiled=True)

    heads = w_proj[:1024].reshape(4, 16, 4, 4, 256).transpose(2, 0, 1, 3, 4).reshape(4, 256, 256)
    biases = b_branch[:4].reshape(4, 16, 4, 4).transpose(2, 0, 1, 3).reshape(4, 256)
    blend = blend_matrix(row_index, row_count, tile_index, tile_count)
    context, decoded = pl.pallas_call(
        tail_kernel,
        name="decoder",
        out_shape=(
            jax.ShapeDtypeStruct((4, 16, 256), BF),
            jax.ShapeDtypeStruct((16, 64, 256), BF),
        ),
        in_specs=[on_chip] * 11,
        out_specs=(on_chip, on_chip),
        scratch_shapes=[
            pltpu.VMEM((PIECE, 256), F32),
            pltpu.VMEM((128, 256), BF),
            pltpu.VMEM((3, EXT, 64, 256), BF),
        ],
    )(
        received,
        heads,
        w_proj[1024:],
        biases,
        b_branch[4:5],
        b_proj[None],
        blend,
        low_taps,
        w_dec_up,
        w_dec_low.reshape(3, 144, 256),
        b_dec[None],
    )
    return (context, decoded)


def solution(mesh):
    names = [name for name, size in SPLIT]
    sizes = [size for name, size in SPLIT]
    fine_mesh = Mesh(mesh.devices.reshape(sizes), names)
    in_specs = (
        P(ROWS, None, CHAN),
        P(ROWS, CHAN, None),
        P(CHAN, None),
        P(None, None, CHAN, ROWS),
        P(CHAN, None),
        P(),
        P(),
        P(),
        P(),
        P(),
        P(),
        P(),
        P(),
    )
    out_specs = (P(ROWS, CHAN, None), P(ROWS, CHAN, None))
    return jax.shard_map(
        on_device, mesh=fine_mesh, in_specs=in_specs, out_specs=out_specs, check_vma=False
    )
```

time: 450 us -> 163 us (0.36); the launches traced: 444 us -> 162 us
  waiting for transfers between devices: 141 us -> 19.9 us
  blocking collectives: 143 us -> 38.6 us
  local copies, waits for them, and re-layouts: 64.6 us -> 20.1 us
  Pallas kernels: 0 us -> 21.9 us
  matrix products: 15.1 us -> 0.27 us
  between operations: 14.8 us -> 1.05 us
  starting transfers between devices: 60.4 us -> 49.9 us
  other arithmetic: 4.84 us -> 10.3 us
    psum x2 -> x0, blocking collectives: 143 us -> none  [the longest x1 129 us: on_device(): pooled = lax.psum(local_sum, 'rows') / map_total]
    all_gather x1 -> x0, waiting for transfers between devices: 108 us -> none  [on_device(): rate_all = lax.all_gather(w_rate, 'rows', axis=3, tiled=True)]
    all_gather x0 -> x1, blocking collectives: none -> 38.6 us  [on_device(): packed = lax.all_gather(unit, 'z', axis=0, tiled=True)]
    unnamed x92 -> x49, local copies, waits for them, and re-layouts: 37.6 us -> 12.2 us
    ppermute x18 -> x10, starting transfers between devices: 60.3 us -> 35.8 us  [the longest x1 5.77 us: on_device(): across_y = lax.ppermute(features, 'yh', swap('yh'))]
    pallas_call x0 -> x2, Pallas kernels: none -> 21.9 us  [the longest x1 15.9 us: on_device(): pl.pallas_call(conv_kernel, name='branches', out_shape=jax.ShapeDtypeStru...]
    reduce_scatter x1 -> x0, waiting for transfers between devices: 20.5 us -> none  [on_device(): lax.psum_scatter(partial_terms.astype(jnp.bfloat16), 'chan', scatter_dime...]
    slice x19 -> x7, local copies, waits for them, and re-layouts: 18.1 us -> 1.51 us  [the longest x1 0.65 us: on_device(): w_proj[1024:]]
  transfers between devices with their start and end apart: 21 -> 11, of which waited for: 7 -> 2; matrix products, arithmetic and copies ran while one was open for 4% -> 17% of each run, Pallas kernels for 0% -> 0%
where the time goes in v1:
time: 163 us; the launch traced here: 162 us
  starting transfers between devices  49.9 us (31%)
  blocking collectives  38.6 us (24%)
  Pallas kernels  21.9 us (13%)
  local copies, waits for them, and re-layouts  20.1 us (12%)
  waiting for transfers between devices  19.9 us (12%)
  other arithmetic  10.3 us (6%)
    all_gather x1, blocking collectives, on_device(): packed = lax.all_gather(unit, 'z', axis=0, tiled=True)  38.6 us
    ppermute x1, waiting for transfers between devices, on_device(): left = lax.ppermute(low_mapped[:, 63:], CHAN, shift_pairs(tile_count, 1))  18.5 us
    pallas_call x1, Pallas kernels, on_device(): pl.pallas_call(conv_kernel, name='branches', out_shape=jax.ShapeDtypeStru...  15.9 us
    all_to_all x1, starting transfers between devices, on_device(): received = lax.all_to_all(pieces, BLOCK, 0, 0, tiled=True)  14.1 us
    unnamed x49, local copies, waits for them, and re-layouts  12.2 us
    pallas_call x1, Pallas kernels, on_device(): pl.pallas_call(tail_kernel, name='decoder', out_shape=(jax.ShapeDtypeStru...  6.05 us
    ppermute x1, starting transfers between devices, on_device(): across_y = lax.ppermute(features, 'yh', swap('yh'))  5.77 us
    ppermute x1, starting transfers between devices, on_device(): above = lax.ppermute(eight, 'z', shift_pairs(z_count, 1))  4.95 us
  transfers between devices with their start and end apart: 11, of which 2 were waited for; matrix products, arithmetic and copies ran while one was open for 17% of the time, Pallas kernels for 0%

profile of v1, /device:TPU:1, one launch (start us, length us, event | category | flops | bytes accessed | tf_op | source)
XLA Modules:
  0.0 162.1 jit_solution(15167743948820894121)
XLA Ops:
  0.7 5.8 %collective-permute-start = (bf16[4,128,256]{2,1,0:T(8,128)(2,1)}, bf16[4,128,256]{2,1,0:T(8,128)(2,1)S(1)}, u32[]{:S(2)}, u32[]{:S(2)}) collective-permute-start(bf16[4,128,256]{2,1,0:T(8,128)(2,1)} %param.25), channel_id=1, source_target_pairs={{0,16},{16,0},{1,17},{17,1},{2,18},{18,2},{3,19},{19,3},{4,20},{20... | collective-permute-start | bytes 786440 | tf_op jit(solution)/shard_map/ppermute | solution.py:258
  7.5 1.4 select_select_fusion.2
  9.6 1.4 select_select_fusion
  12.2 4.9 %collective-permute-start.2 = (bf16[8,128,256]{2,1,0:T(8,128)(2,1)S(1)}, bf16[8,128,256]{2,1,0:T(8,128)(2,1)S(1)}, u32[]{:S(2)}, u32[]{:S(2)}) collective-permute-start(bf16[8,128,256]{2,1,0:T(8,128)(2,1)S(1)} %maximum_select_fusion.eight), channel_id=1, source_target_pairs={{0,32},{32,64},{64,96},{96,128},{128,160},{160,192},{192,224},{224... | collective-permute-start | bytes 1572872 | tf_op jit(solution)/shard_map/ppermute | solution.py:265
  17.1 1.3 collective-permute-start.3
  18.4 4.9 %collective-permute-start.1 = (bf16[8,128,256]{2,1,0:T(8,128)(2,1)S(1)}, bf16[8,128,256]{2,1,0:T(8,128)(2,1)}, u32[]{:S(2)}, u32[]{:S(2)}) collective-permute-start(bf16[8,128,256]{2,1,0:T(8,128)(2,1)S(1)} %maximum_select_fusion.eight), channel_id=1, source_target_pairs={{0,8},{8,0},{1,9},{9,1},{2,10},{10,2},{3,11},{11,3},{4,12},{12,4},... | collective-permute-start | bytes 1572872 | tf_op jit(solution)/shard_map/ppermute | solution.py:270
  28.7 4.5 %collective-permute-start.4 = (bf16[3,128,256]{2,1,0:T(8,128)(2,1)S(1)}, bf16[3,128,256]{2,1,0:T(8,128)(2,1)S(1)}, u32[]{:S(2)}, u32[]{:S(2)}) collective-permute-start(bf16[3,128,256]{2,1,0:T(8,128)(2,1)S(1)} %slice_select_fusion), channel_id=1, source_target_pairs={{8,72},{40,104},{72,136},{104,168},{136,200},{168,232},{200,264},{... | collective-permute-start | bytes 589832 | tf_op jit(solution)/shard_map/ppermute | solution.py:269
  34.4 1.4 collective-permute-done.4.far
  35.8 1.3 pad_maximum_fusion
  37.2 3.3 %collective-permute-start.5 = (bf16[19,128,256]{2,1,0:T(8,128)(2,1)}, bf16[19,128,256]{2,1,0:T(8,128)(2,1)S(1)}, u32[]{:S(2)}, u32[]{:S(2)}) collective-permute-start(bf16[19,128,256]{2,1,0:T(8,128)(2,1)} %pad_maximum_fusion), channel_id=1, source_target_pairs={{0,8},{8,0},{1,9},{9,1},{2,10},{10,2},{3,11},{11,3},{4,12},{12,4},... | collective-permute-start | bytes 3735560 | tf_op jit(solution)/shard_map/ppermute | solution.py:295
  41.8 1.3 constant_dynamic-update-slice_fusion.2
  43.1 1.3 constant_dynamic-update-slice_fusion.1
  44.3 1.3 constant_dynamic-update-slice_fusion
  46.4 38.6 %all_gather.3.packed = bf16[16,120,256]{2,1,0:T(8,128)(2,1)} all-gather(bf16[1,120,256]{2,1,0:T(8,128)(2,1)S(1)} %reshape.188), channel_id=1, replica_groups=mesh['z'=16,'yh'=2,'core'=2,'x'=4,'yl'=2] {'z'}, dimensions={0}, use_global_device_ids=true | all-gather | bytes 1044480 | tf_op jit(solution)/shard_map/all_gather | solution.py:293
  86.1 15.9 %branches.1 = bf16[32,112,256]{2,1,0:T(8,128)(2,1)} custom-call(s32[2]{0:T(128)} %pad_add_fusion.place, bf16[8,128,256]{2,1,0:T(8,128)(2,1)} %copy-done.2, bf16[8,128,256]{2,1,0:T(8,128)(2,1)} %collective-permute-done.1.other, bf16[8,128,256]{2,1,0:T(8,128)(2,1)} %copy-done.3, bf16[8,128,256]{2,1,0:T(8,128)(2,1)} %copy-done.4, ...), custom_call_target="tpu_custom_call" | custom-call | tf_op jit(solution)/shard_map/branches/pallas_call | solution.py:300
  102.1 14.1 %all-to-all-start = ((bf16[32,112,256]{2,1,0:T(8,128)(2,1)}), bf16[32,112,256]{2,1,0:T(8,128)(2,1)S(1)}, u32[]{:S(2)}, u32[]{:S(2)}) async-start(bf16[32,112,256]{2,1,0:T(8,128)(2,1)} %branches.1), calls=%async_computation | async-start | bytes 3670016 | tf_op jit(solution)/shard_map/all_to_all | solution.py:314
  116.8 3.3 %collective-permute-start.6 = (bf16[16,1,48]{2,1,0:T(2,128)(2,1)S(1)}, bf16[16,1,48]{2,1,0:T(2,128)(2,1)S(1)}, u32[]{:S(2)}, u32[]{:S(2)}) collective-permute-start(bf16[16,1,48]{2,1,0:T(2,128)(2,1)S(1)} %get-tuple-element.13), channel_id=1, source_target_pairs={{0,1},{1,2},{2,3},{3,4},{4,5},{5,6},{6,7},{8,9},{9,10},{10,11},{11... | collective-permute-start | bytes 4616 | tf_op jit(solution)/shard_map/ppermute | solution.py:275
  120.0 1.3 collective-permute-start.7
  121.6 18.5 %collective-permute-done.6 = bf16[16,1,48]{2,1,0:T(2,128)(2,1)S(1)} collective-permute-done((bf16[16,1,48]{2,1,0:T(2,128)(2,1)S(1)}, bf16[16,1,48]{2,1,0:T(2,128)(2,1)S(1)}, u32[]{:S(2)}, u32[]{:S(2)}) %collective-permute-start.6) | collective-permute-done | bytes 1568 | tf_op jit(solution)/shard_map/ppermute | solution.py:275
  140.1 4.7 %collective-permute-start.8 = (bf16[1,66,48]{2,1,0:T(8,128)(2,1)S(1)}, bf16[1,66,48]{2,1,0:T(8,128)(2,1)S(1)}, u32[]{:S(2)}, u32[]{:S(2)}) collective-permute-start(bf16[1,66,48]{2,1,0:T(8,128)(2,1)S(1)} %get-tuple-element.11), channel_id=1, source_target_pairs={{0,8},{8,16},{16,24},{24,32},{32,40},{40,48},{48,56},{56,64},{64,7... | collective-permute-start | bytes 19016 | tf_op jit(solution)/shard_map/ppermute | solution.py:278
  144.8 1.9 %collective-permute-start.9 = (bf16[1,66,48]{2,1,0:T(8,128)(2,1)S(1)}, bf16[1,66,48]{2,1,0:T(8,128)(2,1)S(1)}, u32[]{:S(2)}, u32[]{:S(2)}) collective-permute-start(bf16[1,66,48]{2,1,0:T(8,128)(2,1)S(1)} %get-tuple-element.12), channel_id=1, source_target_pairs={{8,0},{16,8},{24,16},{32,24},{40,32},{48,40},{56,48},{64,56},{72,6... | collective-permute-start | bytes 19016 | tf_op jit(solution)/shard_map/ppermute | solution.py:279
  150.0 1.3 copy.37
  153.5 1.3 pad_maximum_fusion.2.low
  156.0 6.0 %decoder.1 = (bf16[4,16,256]{2,1,0:T(8,128)(2,1)}, bf16[16,64,256]{2,1,0:T(8,128)(2,1)}) custom-call(bf16[32,112,256]{2,1,0:T(8,128)(2,1)} %copy-done.1, bf16[4,256,256]{2,1,0:T(8,128)(2,1)} %reshape.190.w_proj, bf16[256,256]{1,0:T(8,128)(2,1)} %slice.90.w_head, f32[4,256]{1,0:T(4,128)} %reshape.192.b_branch, f32[1,256]{1,0:T(1,128)} %slice.92.b_pool, ...), custom_call_target="tpu_custom_call" | custom-call | tf_op jit(solution)/shard_map/decoder/pallas_call | solution.py:319
  (83 shorter events, 20.2 us)
Async XLA Ops:
  0.6 115.6 %copy-start = (bf16[16,64,256]{2,1,0:T(8,128)(2,1)S(1)}, bf16[16,64,256]{2,1,0:T(8,128)(2,1)}, u32[]{:S(2)}) copy-start(bf16[16,64,256]{2,1,0:T(8,128)(2,1)} %param.26) | copy-start | bytes 1572868
  0.6 22.6 %copy-start.11 = (bf16[3,9,256,4]{2,3,1,0:T(4,128)(2,1)S(1)}, bf16[3,9,256,4]{2,3,1,0:T(4,128)(2,1)}, u32[]{:S(2)}) copy-start(bf16[3,9,256,4]{2,3,1,0:T(4,128)(2,1)} %param.28) | copy-start | bytes 165892
  0.7 10.4 %collective-permute-start = (bf16[4,128,256]{2,1,0:T(8,128)(2,1)}, bf16[4,128,256]{2,1,0:T(8,128)(2,1)S(1)}, u32[]{:S(2)}, u32[]{:S(2)}) collective-permute-start(bf16[4,128,256]{2,1,0:T(8,128)(2,1)} %param.25), channel_id=1, source_target_pairs={{0,16},{16,0},{1,17},{17,1},{2,18},{18,2},{3,19},{19,3},{4,20},{20... | collective-permute-start | bytes 786440 | tf_op jit(solution)/shard_map/ppermute | solution.py:258
  12.2 25.0 %copy-start.2 = (bf16[8,128,256]{2,1,0:T(8,128)(2,1)}, bf16[8,128,256]{2,1,0:T(8,128)(2,1)S(1)}, u32[]{:S(2)}) copy-start(bf16[8,128,256]{2,1,0:T(8,128)(2,1)S(1)} %maximum_select_fusion.eight) | copy-start | bytes 1572868
  12.2 23.6 %collective-permute-start.2 = (bf16[8,128,256]{2,1,0:T(8,128)(2,1)S(1)}, bf16[8,128,256]{2,1,0:T(8,128)(2,1)S(1)}, u32[]{:S(2)}, u32[]{:S(2)}) collective-permute-start(bf16[8,128,256]{2,1,0:T(8,128)(2,1)S(1)} %maximum_select_fusion.eight), channel_id=1, source_target_pairs={{0,32},{32,64},{64,96},{96,128},{128,160},{160,192},{192,224},{224... | collective-permute-start | bytes 1572872 | tf_op jit(solution)/shard_map/ppermute | solution.py:265
  17.1 18.7 %collective-permute-start.3 = (bf16[8,128,256]{2,1,0:T(8,128)(2,1)S(1)}, bf16[8,128,256]{2,1,0:T(8,128)(2,1)S(1)}, u32[]{:S(2)}, u32[]{:S(2)}) collective-permute-start(bf16[8,128,256]{2,1,0:T(8,128)(2,1)S(1)} %maximum_select_fusion.eight), channel_id=1, source_target_pairs={{32,0},{64,32},{96,64},{128,96},{160,128},{192,160},{224,192},{256... | collective-permute-start | bytes 1572872 | tf_op jit(solution)/shard_map/ppermute | solution.py:266
  18.4 66.6 %collective-permute-start.1 = (bf16[8,128,256]{2,1,0:T(8,128)(2,1)S(1)}, bf16[8,128,256]{2,1,0:T(8,128)(2,1)}, u32[]{:S(2)}, u32[]{:S(2)}) collective-permute-start(bf16[8,128,256]{2,1,0:T(8,128)(2,1)S(1)} %maximum_select_fusion.eight), channel_id=1, source_target_pairs={{0,8},{8,0},{1,9},{9,1},{2,10},{10,2},{3,11},{11,3},{4,12},{12,4},... | collective-permute-start | bytes 1572872 | tf_op jit(solution)/shard_map/ppermute | solution.py:270
  28.7 7.0 %collective-permute-start.4 = (bf16[3,128,256]{2,1,0:T(8,128)(2,1)S(1)}, bf16[3,128,256]{2,1,0:T(8,128)(2,1)S(1)}, u32[]{:S(2)}, u32[]{:S(2)}) collective-permute-start(bf16[3,128,256]{2,1,0:T(8,128)(2,1)S(1)} %slice_select_fusion), channel_id=1, source_target_pairs={{8,72},{40,104},{72,136},{104,168},{136,200},{168,232},{200,264},{... | collective-permute-start | bytes 589832 | tf_op jit(solution)/shard_map/ppermute | solution.py:269
  37.2 47.8 %collective-permute-start.5 = (bf16[19,128,256]{2,1,0:T(8,128)(2,1)}, bf16[19,128,256]{2,1,0:T(8,128)(2,1)S(1)}, u32[]{:S(2)}, u32[]{:S(2)}) collective-permute-start(bf16[19,128,256]{2,1,0:T(8,128)(2,1)} %pad_maximum_fusion), channel_id=1, source_target_pairs={{0,8},{8,0},{1,9},{9,1},{2,10},{10,2},{3,11},{11,3},{4,12},{12,4},... | collective-permute-start | bytes 3735560 | tf_op jit(solution)/shard_map/ppermute | solution.py:295
  102.0 14.2 %copy-start.14 = (f32[18,128]{1,0:T(8,128)S(1)}, f32[18,128]{1,0:T(8,128)}, u32[]{:S(2)}) copy-start(f32[18,128]{1,0:T(8,128)} %constant.64.clone) | copy-start | bytes 27652
  102.0 14.2 %copy-start.15 = (f32[18,128]{1,0:T(8,128)S(1)}, f32[18,128]{1,0:T(8,128)}, u32[]{:S(2)}) copy-start(f32[18,128]{1,0:T(8,128)} %constant.65.clone) | copy-start | bytes 27652
  102.0 14.2 %copy-start.16 = (f32[18,128]{1,0:T(8,128)S(1)}, f32[18,128]{1,0:T(8,128)}, u32[]{:S(2)}) copy-start(f32[18,128]{1,0:T(8,128)} %constant.66.clone) | copy-start | bytes 27652
  102.0 14.3 %copy-start.12 = (bf16[256,48]{0,1:T(8,128)(2,1)S(1)}, bf16[256,48]{0,1:T(8,128)(2,1)}, u32[]{:S(2)}) copy-start(bf16[256,48]{0,1:T(8,128)(2,1)} %param.33) | copy-start | bytes 73732
  102.0 14.2 %copy-start.17 = (f32[48]{0:T(128)S(1)}, f32[48]{0:T(128)}, u32[]{:S(2)}) copy-start(f32[48]{0:T(128)} %param.34) | copy-start | bytes 580
  102.1 19.3 %copy-start.8 = (f32[64,128]{1,0:T(8,128)S(1)}, f32[64,128]{1,0:T(8,128)}, u32[]{:S(2)}) copy-start(f32[64,128]{1,0:T(8,128)} %select_select_fusion.2) | copy-start | bytes 98308
  102.1 19.3 %copy-start.9 = (f32[64,128]{1,0:T(8,128)S(1)}, f32[64,128]{1,0:T(8,128)}, u32[]{:S(2)}) copy-start(f32[64,128]{1,0:T(8,128)} %get-tuple-element.21) | copy-start | bytes 98308
  102.1 19.3 %copy-start.10 = (f32[64,128]{1,0:T(8,128)S(1)}, f32[64,128]{1,0:T(8,128)}, u32[]{:S(2)}) copy-start(f32[64,128]{1,0:T(8,128)} %get-tuple-element.22) | copy-start | bytes 98308
  102.1 52.7 %all-to-all-start = ((bf16[32,112,256]{2,1,0:T(8,128)(2,1)}), bf16[32,112,256]{2,1,0:T(8,128)(2,1)S(1)}, u32[]{:S(2)}, u32[]{:S(2)}) async-start(bf16[32,112,256]{2,1,0:T(8,128)(2,1)} %branches.1), calls=%async_computation | async-start | bytes 3670016 | tf_op jit(solution)/shard_map/all_to_all | solution.py:314
  116.8 23.3 %collective-permute-start.6 = (bf16[16,1,48]{2,1,0:T(2,128)(2,1)S(1)}, bf16[16,1,48]{2,1,0:T(2,128)(2,1)S(1)}, u32[]{:S(2)}, u32[]{:S(2)}) collective-permute-start(bf16[16,1,48]{2,1,0:T(2,128)(2,1)S(1)} %get-tuple-element.13), channel_id=1, source_target_pairs={{0,1},{1,2},{2,3},{3,4},{4,5},{5,6},{6,7},{8,9},{9,10},{10,11},{11... | collective-permute-start | bytes 4616 | tf_op jit(solution)/shard_map/ppermute | solution.py:275
  120.0 20.1 %collective-permute-start.7 = (bf16[16,1,48]{2,1,0:T(2,128)(2,1)S(1)}, bf16[16,1,48]{2,1,0:T(2,128)(2,1)S(1)}, u32[]{:S(2)}, u32[]{:S(2)}) collective-permute-start(bf16[16,1,48]{2,1,0:T(2,128)(2,1)S(1)} %get-tuple-element.14), channel_id=1, source_target_pairs={{1,0},{2,1},{3,2},{4,3},{5,4},{6,5},{7,6},{9,8},{10,9},{11,10},{12... | collective-permute-start | bytes 4616 | tf_op jit(solution)/shard_map/ppermute | solution.py:276
  121.6 26.2 %copy-start.7 = (bf16[1280,256]{1,0:T(8,128)(2,1)S(1)}, bf16[1280,256]{1,0:T(8,128)(2,1)}, u32[]{:S(2)}) copy-start(bf16[1280,256]{1,0:T(8,128)(2,1)} %param.31) | copy-start | bytes 1966084
  140.1 13.0 %collective-permute-start.8 = (bf16[1,66,48]{2,1,0:T(8,128)(2,1)S(1)}, bf16[1,66,48]{2,1,0:T(8,128)(2,1)S(1)}, u32[]{:S(2)}, u32[]{:S(2)}) collective-permute-start(bf16[1,66,48]{2,1,0:T(8,128)(2,1)S(1)} %get-tuple-element.11), channel_id=1, source_target_pairs={{0,8},{8,16},{16,24},{24,32},{32,40},{40,48},{48,56},{56,64},{64,7... | collective-permute-start | bytes 19016 | tf_op jit(solution)/shard_map/ppermute | solution.py:278
  144.8 8.3 %collective-permute-start.9 = (bf16[1,66,48]{2,1,0:T(8,128)(2,1)S(1)}, bf16[1,66,48]{2,1,0:T(8,128)(2,1)S(1)}, u32[]{:S(2)}, u32[]{:S(2)}) collective-permute-start(bf16[1,66,48]{2,1,0:T(8,128)(2,1)S(1)} %get-tuple-element.12), channel_id=1, source_target_pairs={{8,0},{16,8},{24,16},{32,24},{40,32},{48,40},{56,48},{64,56},{72,6... | collective-permute-start | bytes 19016 | tf_op jit(solution)/shard_map/ppermute | solution.py:279
  150.0 2.2 %slice-start = ((f32[5,256]{1,0:T(8,128)}), f32[4,256]{1,0:T(4,128)S(1)}, s32[]{:S(2)}) async-start(f32[5,256]{1,0:T(8,128)} %param.30), calls=%async_computation.1 | async-start | bytes 8192 | tf_op jit(solution)/shard_map/slice | solution.py:317
  (6 other events, 8.2 us)

commit v2 on v1

--- a/solution.py
+++ b/solution.py
@@ -1,5 +1,3 @@
-import functools
-
 import jax
 import jax.numpy as jnp
 import numpy as np
@@ -20,11 +18,11 @@
 STRIP = 4
 EXT = 18
 REACH = 19
-UNIT = 120
+UNIT = 112
 PIECE = 112
 
 
-def swap(axis):
+def swap():
     return [(0, 1), (1, 0)]
 
 
@@ -43,13 +41,17 @@
     return lax.dot_general(a, b, (((1,), (1,)), ((), ())), preferred_element_type=F32)
 
 
+def held(array):
+    return pltpu.with_memory_space_constraint(array, pltpu.HBM)
+
+
 def dot(a, b):
     return jnp.dot(a, b, preferred_element_type=F32)
 
 
 def conv_kernel(
-    place, eight, other, above, below, far, traded, packed, w_one, w_pool, out,
-    x, rhs, wide, piece, sems,
+    place, mine, theirs, packed, w_one, w_pool, out,
+    x, rhs, wide, piece, ready, sems, out_sems,
 ):
     core = place[0]
     member = place[1]
@@ -63,28 +65,23 @@
         copy.start()
         copies.append(copy)
 
-    for half in range(2):
-        mine = 8 * half + STRIP * core
-        theirs = 8 * half + STRIP * (1 - core)
-        fetch(eight, STRIP * half, STRIP, REACH + mine)
-        fetch(other, STRIP * half, STRIP, REACH + theirs)
-        fetch(above, STRIP * half, STRIP, REACH - 16 + mine)
-        fetch(below, STRIP * half, STRIP, REACH + 16 + mine)
-        fetch(traded, STRIP * half, STRIP, REACH - 16 + theirs)
-        fetch(traded, 8 + STRIP * half, STRIP, REACH + 16 + theirs)
-    fetch(far, 0, 3, 51 * (1 - core))
-    fetch(traded, 16, 3, 51 * core)
+    for part, base in ((0, REACH), (1, REACH - 16), (2, REACH + 16)):
+        for half in range(2):
+            first = 8 * part + STRIP * half
+            fetch(mine, first, STRIP, base + 8 * half + STRIP * core)
+            fetch(theirs, first, STRIP, base + 8 * half + STRIP * (1 - core))
+    fetch(mine, 24, 3, 51 * (1 - core))
+    fetch(theirs, 24, 3, 51 * core)
 
     slot = (lax.broadcasted_iota(jnp.int32, (256, 256), 0) // 4) % 4
-    for level in range(3):
-        for index, (first, low, high) in enumerate(
-            ((4 * level, 0, 2), (12 + 6 * level, 0, 2), (14 + 6 * level, 1, 3))
-        ):
-            rows = packed[:, 4 * first : 4 * first + 16, :].reshape(256, 256).astype(F32)
-            keep = (slot >= low) & (slot <= high)
-            rhs[3 * level + index] = jnp.where(keep, rows, 0.0).astype(BF)
-
-    sums = jnp.sum(packed[:, 24:32, :].astype(F32), axis=0)
+    for index in range(9):
+        odd = index % 2
+        first = 12 * index - 4 * odd
+        rows = packed[:, first : first + 16, :].reshape(256, 256).astype(F32)
+        keep = (slot >= odd) & (slot <= 2 + odd)
+        rhs[index] = jnp.where(keep, rows, 0.0).astype(BF)
+
+    sums = jnp.sum(packed[:, 104:112, :].astype(F32), axis=0)
     pooled = (sums[4:5] + sums[5:6] + sums[6:7]) / float(256 * 128)
     pre = jnp.dot(
         jnp.broadcast_to(pooled, (8, 256)),
@@ -135,32 +132,50 @@
                     jnp.where(from_right, pltpu.roll(value, 128 - spacing, 1), 0.0),
                 ),
             ).reshape(768, 256)
-            high = moved.astype(BF)
-            low = (moved - high.astype(F32)).astype(BF)
-            total += dot(high, picks[level]) + dot(low, picks[level])
+            total += dot(moved.astype(BF), picks[level])
         wide[pl.ds(first, 6), 8:136, :] = total.reshape(6, 128, 256)
         return carry
 
     lax.fori_loop(0, 3, chunk, 0)
 
+    def put(slot, index):
+        return pltpu.make_async_copy(ready.at[slot], out.at[index], out_sems.at[slot])
+
     def send(part, carry):
         for tile in range(8):
+            slot = tile % 2
             for line in range(6):
                 piece[18 * line : 18 * line + 18, :] = wide[
                     STRIP * part + line, 16 * tile + 7 : 16 * tile + 25, :
                 ]
-            out[4 * tile + part] = piece[...].astype(BF)
+            if tile < 2:
+                @pl.when(part > 0)
+                def _():
+                    put(slot, 4 * (tile + 6) + part - 1).wait()
+            else:
+                put(slot, 4 * (tile - 2) + part).wait()
+            ready[slot] = piece[...].astype(BF)
+            put(slot, 4 * tile + part).start()
         return carry
 
     lax.fori_loop(0, 4, send, 0)
+    put(0, 4 * 6 + 3).wait()
+    put(1, 4 * 7 + 3).wait()
 
 
 def tail_kernel(
-    received, w_proj, w_head, b_branch, b_pool, b_proj, blend, low, w_up, w_low, b_dec,
-    context, decoded, cells, coarse, fine,
+    received, heads, w_head, b_branch, b_pool, b_proj, blend, low, ups, lows, b_dec,
+    context, decoded, cells, coarse, fine, w_proj, w_up, w_low, sems,
 ):
+    copies = [
+        pltpu.make_async_copy(source, target, sems.at[index])
+        for index, (source, target) in enumerate(((heads, w_proj), (ups, w_up), (lows, w_low)))
+    ]
+    for copy in copies:
+        copy.start()
     pool = jnp.zeros((4, 256), F32)
     total = jnp.zeros((PIECE, 256), F32)
+    copies[0].wait()
     for part in range(4):
         summed = received[part].astype(F32)
         for tile in range(1, 8):
@@ -181,6 +196,8 @@
         context[line] = cells[18 * line + 19 : 18 * line + 35, :].astype(BF)
     for across in range(3):
         fine[across] = dot(blend[across], coarse[...]).astype(BF).reshape(EXT, 64, 256)
+    copies[1].wait()
+    copies[2].wait()
     for first in (0, 8):
         mixed = jnp.broadcast_to(b_dec[...], (512, 256))
         for down in range(3):
@@ -229,6 +246,20 @@
         )
         blocks.append((rows[:, None, :] * cols[None, :, :]).astype(BF).reshape(EXT * 64, 128))
     return jnp.stack(blocks)
+
+
+def tap_order():
+    table = np.zeros((UNIT, 108), np.float32)
+    taps = []
+    for level in range(3):
+        for part, first in enumerate((3, 0, 6)):
+            first += 9 * level
+            odd = (3 * level + part) % 2
+            taps += [first + 1, first + 2, first] if odd else [first, first + 1, first + 2]
+    for place, tap in enumerate(taps):
+        for channel in range(4):
+            table[4 * place + channel, 4 * tap + channel] = 1.0
+    return table
 
 
 def on_device(
@@ -255,63 +286,70 @@
     tile_index = lax.axis_index(CHAN)
     tile_count = lax.axis_size(CHAN)
 
-    across_y = lax.ppermute(features, "yh", swap("yh"))
-    across_y, w_rate, low_features = lax.optimization_barrier((across_y, w_rate, low_features))
+    across_y = lax.ppermute(features, "yh", swap())
+
+    low_flat = low_features.reshape(-1, low_features.shape[2])
+    low_mapped = jax.nn.relu(jnp.dot(low_flat, w_low, preferred_element_type=F32) + b_low)
+    low_mapped = low_mapped.astype(BF).reshape(16, 64, 48)
+    taps = jnp.transpose(w_rate, (0, 1, 3, 2)).reshape(108, 256)
+    unit = jnp.dot(jnp.asarray(tap_order(), BF), taps, preferred_element_type=F32)
+    high, mid, rest = halves(jnp.sum(features, axis=(0, 1), dtype=F32)[None])
+    line = lax.broadcasted_iota(jnp.int32, (UNIT, 256), 0)
+    for index, value in enumerate((high, mid, rest)):
+        unit = jnp.where(line == 108 + index, value, unit)
+    unit = unit.astype(BF)[None]
+
+    packed = lax.all_gather(unit, "z", axis=0, tiled=True)
+    across_y, packed, low_mapped = lax.optimization_barrier((across_y, packed, low_mapped))
     eight = jnp.where(
         yh == 0,
         jnp.concatenate([features, across_y], axis=0),
         jnp.concatenate([across_y, features], axis=0),
     )
+    ends = jnp.where(
+        core == 1,
+        jnp.where(yh == 0, across_y[1:4], features[1:4]),
+        jnp.where(yh == 0, features[0:3], across_y[0:3]),
+    )
     above = lax.ppermute(eight, "z", shift_pairs(z_count, 1))
     below = lax.ppermute(eight, "z", shift_pairs(z_count, -1))
     pairs = [(2 * i + 1, 2 * i + 5) for i in range(z_count - 2)]
     pairs += [(2 * i + 4, 2 * i) for i in range(z_count - 2)]
-    far = lax.ppermute(jnp.where(core == 1, eight[5:8], eight[0:3]), ("z", "core"), pairs)
-    other = lax.ppermute(eight, "core", swap("core"))
-
-    low_flat = low_features.reshape(-1, low_features.shape[2])
-    low_mapped = jax.nn.relu(jnp.dot(low_flat, w_low, preferred_element_type=F32) + b_low)
-    low_mapped = low_mapped.astype(BF).reshape(16, 64, 48)
+    far = lax.ppermute(ends, ("z", "core"), pairs)
     left = lax.ppermute(low_mapped[:, 63:], CHAN, shift_pairs(tile_count, 1))
     right = lax.ppermute(low_mapped[:, :1], CHAN, shift_pairs(tile_count, -1))
     low_mapped = jnp.concatenate([left, low_mapped, right], axis=1)
-    top = lax.ppermute(low_mapped[15:], ROWS, shift_pairs(row_count, 1))
-    bottom = lax.ppermute(low_mapped[:1], ROWS, shift_pairs(row_count, -1))
-    low_mapped = jnp.concatenate([top, low_mapped, bottom], axis=0)
-    low_taps = jnp.concatenate([low_mapped[:, i : i + 64] for i in range(3)], axis=2)
-
-    taps = jnp.transpose(w_rate, (0, 1, 3, 2))
-    local_sum = jnp.sum(features, axis=(0, 1), dtype=F32)
-    empty = jnp.zeros((1, 4, 256), BF)
-    pool_rows = jnp.stack(halves(local_sum) + (jnp.zeros_like(local_sum),))[None].astype(BF)
-    unit = []
-    for level in range(3):
-        unit += [taps[level, 3:6], pool_rows if level == 1 else empty]
-    for level in range(3):
-        unit += [taps[level, 0:3], taps[level, 7:9], taps[level, 6:7]]
-    unit = jnp.concatenate(unit, axis=0).reshape(1, UNIT, 256)
-    packed = lax.all_gather(unit, "z", axis=0, tiled=True)
-
-    traded = lax.ppermute(jnp.concatenate([above, below, far], axis=0), "core", swap("core"))
+    above, below, far, low_mapped = lax.optimization_barrier((above, below, far, low_mapped))
+    joint = jnp.concatenate([eight, above, below, far], axis=0)
+    traded = lax.ppermute(joint, "core", swap())
 
     place = jnp.stack([core, member]).astype(jnp.int32)
+    on_chip = pl.BlockSpec(memory_space=pltpu.VMEM)
     anywhere = pl.BlockSpec(memory_space=pl.ANY)
-    on_chip = pl.BlockSpec(memory_space=pltpu.VMEM)
+    in_hbm = pl.BlockSpec(memory_space=pltpu.HBM)
     pieces = pl.pallas_call(
         conv_kernel,
         name="branches",
         out_shape=jax.ShapeDtypeStruct((32, PIECE, 256), BF),
-        in_specs=[pl.BlockSpec(memory_space=pltpu.SMEM)] + [anywhere] * 6 + [on_chip] * 3,
-        out_specs=on_chip,
+        in_specs=[pl.BlockSpec(memory_space=pltpu.SMEM)] + [anywhere] * 2 + [on_chip] * 3,
+        out_specs=in_hbm,
         scratch_shapes=[
             pltpu.VMEM((54, 128, 256), BF),
             pltpu.VMEM((9, 256, 256), BF),
             pltpu.VMEM((EXT, 144, 256), F32),
             pltpu.VMEM((PIECE, 256), F32),
+            pltpu.VMEM((2, PIECE, 256), BF),
             pltpu.SemaphoreType.DMA((14,)),
+            pltpu.SemaphoreType.DMA((2,)),
         ],
-    )(place, eight, other, above, below, far, traded, packed, w_one, w_pool)
+        compiler_params=pltpu.CompilerParams(vmem_limit_bytes=28 << 20),
+    )(place, joint, traded, packed, w_one, w_pool)
+    pieces = held(pieces)
     received = lax.all_to_all(pieces, BLOCK, 0, 0, tiled=True)
+    top = lax.ppermute(low_mapped[15:], ROWS, shift_pairs(row_count, 1))
+    bottom = lax.ppermute(low_mapped[:1], ROWS, shift_pairs(row_count, -1))
+    low_mapped = jnp.concatenate([top, low_mapped, bottom], axis=0)
+    low_taps = jnp.concatenate([low_mapped[:, i : i + 64] for i in range(3)], axis=2)
 
     heads = w_proj[:1024].reshape(4, 16, 4, 4, 256).transpose(2, 0, 1, 3, 4).reshape(4, 256, 256)
     biases = b_branch[:4].reshape(4, 16, 4, 4).transpose(2, 0, 1, 3).reshape(4, 256)
@@ -323,24 +361,29 @@
             jax.ShapeDtypeStruct((4, 16, 256), BF),
             jax.ShapeDtypeStruct((16, 64, 256), BF),
         ),
-        in_specs=[on_chip] * 11,
+        in_specs=[on_chip, in_hbm] + [on_chip] * 6 + [in_hbm] * 2 + [on_chip],
         out_specs=(on_chip, on_chip),
         scratch_shapes=[
             pltpu.VMEM((PIECE, 256), F32),
             pltpu.VMEM((128, 256), BF),
             pltpu.VMEM((3, EXT, 64, 256), BF),
+            pltpu.VMEM((4, 256, 256), BF),
+            pltpu.VMEM((9, 256, 256), BF),
+            pltpu.VMEM((3, 144, 256), BF),
+            pltpu.SemaphoreType.DMA((3,)),
         ],
+        compiler_params=pltpu.CompilerParams(vmem_limit_bytes=20 << 20),
     )(
         received,
-        heads,
+        held(heads),
         w_proj[1024:],
         biases,
         b_branch[4:5],
         b_proj[None],
         blend,
         low_taps,
-        w_dec_up,
-        w_dec_low.reshape(3, 144, 256),
+        held(w_dec_up),
+        held(w_dec_low.reshape(3, 144, 256)),
         b_dec[None],
     )
     return (context, decoded)
@@ -366,6 +409,7 @@
         P(),
     )
     out_specs = (P(ROWS, CHAN, None), P(ROWS, CHAN, None))
+
     return jax.shard_map(
         on_device, mesh=fine_mesh, in_specs=in_specs, out_specs=out_specs, check_vma=False
     )

time: 163 us -> 135 us (0.83)
  local copies, waits for them, and re-layouts: 20.1 us -> 3.05 us
  other arithmetic: 10.3 us -> 3.88 us
  starting transfers between devices: 49.9 us -> 44.4 us
  Pallas kernels: 21.9 us -> 26.2 us
  blocking collectives: 38.6 us -> 34.5 us
  matrix products: 0.27 us -> 1.92 us
    ppermute x1, waiting for transfers between devices: 18.5 us -> 0.76 us  [on_device(): left = lax.ppermute(low_mapped[:, 63:], CHAN, shift_pairs(tile_count, 1))]
    ppermute x1, waiting for transfers between devices: 0.01 us -> 14.5 us  [on_device(): top = lax.ppermute(low_mapped[15:], ROWS, shift_pairs(row_count, 1))]
    unnamed x49 -> x40, local copies, waits for them, and re-layouts: 12.2 us -> 0.16 us
    all_to_all x1, starting transfers between devices: 14.1 us -> 5.37 us  [on_device(): received = lax.all_to_all(pieces, BLOCK, 0, 0, tiled=True)]
    ppermute x4 -> x3, starting transfers between devices: 18.4 us -> 24.1 us  [the longest x1 13.7 us: on_device(): traded = lax.ppermute(joint, 'core', swap())]
    pallas_call x1, Pallas kernels: 15.9 us -> 20 us  [on_device(): pl.pallas_call(conv_kernel, name='branches', out_shape=jax.ShapeDtypeStru...]
    all_gather x1, blocking collectives: 38.6 us -> 34.5 us  [on_device(): packed = lax.all_gather(unit, 'z', axis=0, tiled=True)]
    ppermute x1, starting transfers between devices: 4.95 us -> 1.32 us  [on_device(): above = lax.ppermute(eight, 'z', shift_pairs(z_count, 1))]
  transfers between devices with their start and end apart: 11 -> 10, of which waited for: 2 -> 4; matrix products, arithmetic and copies ran while one was open for 17% -> 6% of each run, Pallas kernels for 0% -> 0%
where the time goes in v2:
time: 135 us; the launch traced here: 134 us
  starting transfers between devices  44.4 us (33%)
  blocking collectives  34.5 us (26%)
  Pallas kernels  26.2 us (19%)
  waiting for transfers between devices  19 us (14%)
  other arithmetic  3.88 us (3%)
  local copies, waits for them, and re-layouts  3.05 us (2%)
  matrix products  1.92 us (1%)
    all_gather x1, blocking collectives, on_device(): packed = lax.all_gather(unit, 'z', axis=0, tiled=True)  34.5 us
    pallas_call x1, Pallas kernels, on_device(): pl.pallas_call(conv_kernel, name='branches', out_shape=jax.ShapeDtypeStru...  20 us
    ppermute x1, waiting for transfers between devices, on_device(): top = lax.ppermute(low_mapped[15:], ROWS, shift_pairs(row_count, 1))  14.5 us
    ppermute x1, starting transfers between devices, on_device(): traded = lax.ppermute(joint, 'core', swap())  13.7 us
    pallas_call x1, Pallas kernels, on_device(): pl.pallas_call(tail_kernel, name='decoder', out_shape=(jax.ShapeDtypeStru...  6.19 us
    ppermute x1, starting transfers between devices, on_device(): across_y = lax.ppermute(features, 'yh', swap())  5.77 us
    all_to_all x1, starting transfers between devices, on_device(): received = lax.all_to_all(pieces, BLOCK, 0, 0, tiled=True)  5.37 us
    ppermute x1, starting transfers between devices, on_device(): top = lax.ppermute(low_mapped[15:], ROWS, shift_pairs(row_count, 1))  5.18 us
  transfers between devices with their start and end apart: 10, of which 4 were waited for; matrix products, arithmetic and copies ran while one was open for 6% of the time, Pallas kernels for 0%

profile of v2, /device:TPU:1, one launch (start us, length us, event | category | flops | bytes accessed | tf_op | source)
XLA Modules:
  0.0 134.2 jit_solution(5643327700846307959)
XLA Ops:
  0.7 5.8 %collective-permute-start = (bf16[4,128,256]{2,1,0:T(8,128)(2,1)}, bf16[4,128,256]{2,1,0:T(8,128)(2,1)S(1)}, u32[]{:S(2)}, u32[]{:S(2)}) collective-permute-start(bf16[4,128,256]{2,1,0:T(8,128)(2,1)} %param.26), channel_id=1, source_target_pairs={{0,16},{16,0},{1,17},{17,1},{2,18},{18,2},{3,19},{19,3},{4,20},{20... | collective-permute-start | bytes 786440 | tf_op jit(solution)/shard_map/ppermute | solution.py:289
  6.4 1.0 convert_reduce_fusion
  7.5 0.8 reshape.125
  8.4 1.0 fusion.1
  9.6 0.9 fusion.4
  10.5 34.5 %all-gather = bf16[1792,256]{1,0:T(8,128)(2,1)S(1)} all-gather(bf16[112,256]{1,0:T(8,128)(2,1)S(1)} %fusion.4), channel_id=2, replica_groups=mesh['z'=16,'yh'=2,'core'=2,'x'=4,'yl'=2] {'z'}, dimensions={0}, use_global_device_ids=true | all-gather | bytes 974848 | tf_op jit(solution)/shard_map/all_gather | solution.py:302
  45.1 1.3 collective-permute-start.1
  46.4 1.3 collective-permute-start.2
  47.7 4.6 %collective-permute-start.3 = (bf16[3,128,256]{2,1,0:T(8,128)(2,1)S(1)}, bf16[3,128,256]{2,1,0:T(8,128)(2,1)S(1)}, u32[]{:S(2)}, u32[]{:S(2)}) collective-permute-start(bf16[3,128,256]{2,1,0:T(8,128)(2,1)S(1)} %select_select_fusion), channel_id=1, source_target_pairs={{8,72},{40,104},{72,136},{104,168},{136,200},{168,232},{200,264},{... | collective-permute-start | bytes 589832 | tf_op jit(solution)/shard_map/ppermute | solution.py:318
  52.3 1.3 collective-permute-start.5
  53.6 4.0 %collective-permute-start.4 = (bf16[16,1,48]{2,1,0:T(2,128)(2,1)S(1)}, bf16[16,1,48]{2,1,0:T(2,128)(2,1)S(1)}, u32[]{:S(2)}, u32[]{:S(2)}) collective-permute-start(bf16[16,1,48]{2,1,0:T(2,128)(2,1)S(1)} %get-tuple-element.21), channel_id=1, source_target_pairs={{0,1},{1,2},{2,3},{3,4},{4,5},{5,6},{6,7},{8,9},{9,10},{10,11},{11... | collective-permute-start | bytes 4616 | tf_op jit(solution)/shard_map/ppermute | solution.py:319
  57.6 0.8 collective-permute-done.4
  58.4 0.8 pad_maximum_fusion.3
  59.5 13.7 %collective-permute-start.6 = (bf16[27,128,256]{2,1,0:T(8,128)(2,1)S(1)}, bf16[27,128,256]{2,1,0:T(8,128)(2,1)}, u32[]{:S(2)}, u32[]{:S(2)}) collective-permute-start(bf16[27,128,256]{2,1,0:T(8,128)(2,1)S(1)} %pad_maximum_fusion.mine), channel_id=1, source_target_pairs={{0,8},{8,0},{1,9},{9,1},{2,10},{10,2},{3,11},{11,3},{4,12},{12,4},... | collective-permute-start | bytes 5308424 | tf_op jit(solution)/shard_map/ppermute | solution.py:324
  73.4 0.8 select_select_fusion.3
  74.1 2.6 %collective-permute-done.6.theirs = bf16[27,128,256]{2,1,0:T(8,128)(2,1)} collective-permute-done((bf16[27,128,256]{2,1,0:T(8,128)(2,1)S(1)}, bf16[27,128,256]{2,1,0:T(8,128)(2,1)}, u32[]{:S(2)}, u32[]{:S(2)}) %collective-permute-start.6) | collective-permute-done | bytes 1769504 | tf_op jit(solution)/shard_map/ppermute | solution.py:324
  76.7 20.0 %branches.1 = bf16[32,112,256]{2,1,0:T(8,128)(2,1)} custom-call(s32[2]{0:T(128)S(1)} %pad_add_fusion.place, bf16[27,128,256]{2,1,0:T(8,128)(2,1)S(1)} %pad_maximum_fusion.mine, bf16[27,128,256]{2,1,0:T(8,128)(2,1)} %collective-permute-done.6.theirs, bf16[16,112,256]{2,1,0:T(8,128)(2,1)S(1)} %bitcast.23, bf16[256,256]{1,0:T(8,128)(2,1)S(1)} %copy-done.1, ...), custom_call_target="tpu_custom_call" | custom-call | tf_op jit(solution)/shard_map/branches/pallas_call | solution.py:330
  96.8 5.4 %all-to-all-start = ((bf16[32,112,256]{2,1,0:T(8,128)(2,1)}), bf16[32,112,256]{2,1,0:T(8,128)(2,1)}, u32[]{:S(2)}, u32[]{:S(2)}) async-start(bf16[32,112,256]{2,1,0:T(8,128)(2,1)} %branches.1), calls=%async_computation | async-start | bytes 3670016 | tf_op jit(solution)/shard_map/all_to_all | solution.py:348
  102.6 5.2 %collective-permute-start.7 = (bf16[1,66,48]{2,1,0:T(8,128)(2,1)S(1)}, bf16[1,66,48]{2,1,0:T(8,128)(2,1)S(1)}, u32[]{:S(2)}, u32[]{:S(2)}) collective-permute-start(bf16[1,66,48]{2,1,0:T(8,128)(2,1)S(1)} %get-tuple-element.20), channel_id=1, source_target_pairs={{0,8},{8,16},{16,24},{24,32},{32,40},{40,48},{48,56},{56,64},{64,7... | collective-permute-start | bytes 19016 | tf_op jit(solution)/shard_map/ppermute | solution.py:349
  108.4 0.9 reshape.129.heads
  109.6 1.9 %collective-permute-start.8 = (bf16[1,66,48]{2,1,0:T(8,128)(2,1)S(1)}, bf16[1,66,48]{2,1,0:T(8,128)(2,1)S(1)}, u32[]{:S(2)}, u32[]{:S(2)}) collective-permute-start(bf16[1,66,48]{2,1,0:T(8,128)(2,1)S(1)} %get-tuple-element.19), channel_id=1, source_target_pairs={{8,0},{16,8},{24,16},{32,24},{40,32},{48,40},{56,48},{64,56},{72,6... | collective-permute-start | bytes 19016 | tf_op jit(solution)/shard_map/ppermute | solution.py:350
  111.6 14.5 %collective-permute-done.7 = bf16[1,66,48]{2,1,0:T(8,128)(2,1)S(1)} collective-permute-done((bf16[1,66,48]{2,1,0:T(8,128)(2,1)S(1)}, bf16[1,66,48]{2,1,0:T(8,128)(2,1)S(1)}, u32[]{:S(2)}, u32[]{:S(2)}) %collective-permute-start.7) | collective-permute-done | bytes 6368 | tf_op jit(solution)/shard_map/ppermute | solution.py:349
  126.2 1.1 collective-permute-done.8
  128.0 6.2 %decoder.1 = (bf16[4,16,256]{2,1,0:T(8,128)(2,1)}, bf16[16,64,256]{2,1,0:T(8,128)(2,1)}) custom-call(bf16[32,112,256]{2,1,0:T(8,128)(2,1)} %all-to-all-done.received, bf16[4,256,256]{2,1,0:T(8,128)(2,1)} %reshape.129.heads, bf16[256,256]{1,0:T(8,128)(2,1)S(1)} %slice.52.w_head, f32[4,256]{1,0:T(4,128)S(1)} %reshape.131.b_branch, f32[1,256]{1,0:T(1,128)S(1)} %slice.54.b_pool, ...), custom_call_target="tpu_custom_call" | custom-call | tf_op jit(solution)/shard_map/decoder/pallas_call | solution.py:357
  (74 shorter events, 2.5 us)
Async XLA Ops:
  0.6 7.7 %copy-start = (bf16[16,64,256]{2,1,0:T(8,128)(2,1)S(1)}, bf16[16,64,256]{2,1,0:T(8,128)(2,1)}, u32[]{:S(2)}) copy-start(bf16[16,64,256]{2,1,0:T(8,128)(2,1)} %param.27) | copy-start | bytes 1572868
  0.6 44.3 %copy-start.5 = (bf16[4,128,256]{2,1,0:T(8,128)(2,1)S(1)}, bf16[4,128,256]{2,1,0:T(8,128)(2,1)}, u32[]{:S(2)}) copy-start(bf16[4,128,256]{2,1,0:T(8,128)(2,1)} %param.26) | copy-start | bytes 786436
  0.7 44.3 %collective-permute-start = (bf16[4,128,256]{2,1,0:T(8,128)(2,1)}, bf16[4,128,256]{2,1,0:T(8,128)(2,1)S(1)}, u32[]{:S(2)}, u32[]{:S(2)}) collective-permute-start(bf16[4,128,256]{2,1,0:T(8,128)(2,1)} %param.26), channel_id=1, source_target_pairs={{0,16},{16,0},{1,17},{17,1},{2,18},{18,2},{3,19},{19,3},{4,20},{20... | collective-permute-start | bytes 786440 | tf_op jit(solution)/shard_map/ppermute | solution.py:289
  45.1 14.2 %collective-permute-start.1 = (bf16[8,128,256]{2,1,0:T(8,128)(2,1)S(1)}, bf16[8,128,256]{2,1,0:T(8,128)(2,1)S(1)}, u32[]{:S(2)}, u32[]{:S(2)}) collective-permute-start(bf16[8,128,256]{2,1,0:T(8,128)(2,1)S(1)} %maximum_select_fusion), channel_id=1, source_target_pairs={{0,32},{32,64},{64,96},{96,128},{128,160},{160,192},{192,224},{224... | collective-permute-start | bytes 1572872 | tf_op jit(solution)/shard_map/ppermute | solution.py:314
  46.4 12.9 %collective-permute-start.2 = (bf16[8,128,256]{2,1,0:T(8,128)(2,1)S(1)}, bf16[8,128,256]{2,1,0:T(8,128)(2,1)S(1)}, u32[]{:S(2)}, u32[]{:S(2)}) collective-permute-start(bf16[8,128,256]{2,1,0:T(8,128)(2,1)S(1)} %maximum_select_fusion), channel_id=1, source_target_pairs={{32,0},{64,32},{96,64},{128,96},{160,128},{192,160},{224,192},{256... | collective-permute-start | bytes 1572872 | tf_op jit(solution)/shard_map/ppermute | solution.py:315
  47.7 11.5 %collective-permute-start.3 = (bf16[3,128,256]{2,1,0:T(8,128)(2,1)S(1)}, bf16[3,128,256]{2,1,0:T(8,128)(2,1)S(1)}, u32[]{:S(2)}, u32[]{:S(2)}) collective-permute-start(bf16[3,128,256]{2,1,0:T(8,128)(2,1)S(1)} %select_select_fusion), channel_id=1, source_target_pairs={{8,72},{40,104},{72,136},{104,168},{136,200},{168,232},{200,264},{... | collective-permute-start | bytes 589832 | tf_op jit(solution)/shard_map/ppermute | solution.py:318
  52.3 5.3 %collective-permute-start.5 = (bf16[16,1,48]{2,1,0:T(2,128)(2,1)S(1)}, bf16[16,1,48]{2,1,0:T(2,128)(2,1)S(1)}, u32[]{:S(2)}, u32[]{:S(2)}) collective-permute-start(bf16[16,1,48]{2,1,0:T(2,128)(2,1)S(1)} %get-tuple-element.22), channel_id=1, source_target_pairs={{1,0},{2,1},{3,2},{4,3},{5,4},{6,5},{7,6},{9,8},{10,9},{11,10},{12... | collective-permute-start | bytes 4616 | tf_op jit(solution)/shard_map/ppermute | solution.py:320
  53.6 4.8 %collective-permute-start.4 = (bf16[16,1,48]{2,1,0:T(2,128)(2,1)S(1)}, bf16[16,1,48]{2,1,0:T(2,128)(2,1)S(1)}, u32[]{:S(2)}, u32[]{:S(2)}) collective-permute-start(bf16[16,1,48]{2,1,0:T(2,128)(2,1)S(1)} %get-tuple-element.21), channel_id=1, source_target_pairs={{0,1},{1,2},{2,3},{3,4},{4,5},{5,6},{6,7},{8,9},{9,10},{10,11},{11... | collective-permute-start | bytes 4616 | tf_op jit(solution)/shard_map/ppermute | solution.py:319
  59.2 14.1 %copy-start.8 = (f32[64,128]{1,0:T(8,128)S(1)}, f32[64,128]{1,0:T(8,128)}, u32[]{:S(2)}) copy-start(f32[64,128]{1,0:T(8,128)} %constant.74.clone) | copy-start | bytes 98308
  59.2 17.4 %copy-start.1 = (bf16[256,256]{1,0:T(8,128)(2,1)S(1)}, bf16[256,256]{1,0:T(8,128)(2,1)}, u32[]{:S(2)}) copy-start(bf16[256,256]{1,0:T(8,128)(2,1)} %w_one.1) | copy-start | bytes 393220
  59.2 17.4 %copy-start.2 = (bf16[256,256]{1,0:T(8,128)(2,1)S(1)}, bf16[256,256]{1,0:T(8,128)(2,1)}, u32[]{:S(2)}) copy-start(bf16[256,256]{1,0:T(8,128)(2,1)} %w_pool.1) | copy-start | bytes 393220
  59.5 17.2 %collective-permute-start.6 = (bf16[27,128,256]{2,1,0:T(8,128)(2,1)S(1)}, bf16[27,128,256]{2,1,0:T(8,128)(2,1)}, u32[]{:S(2)}, u32[]{:S(2)}) collective-permute-start(bf16[27,128,256]{2,1,0:T(8,128)(2,1)S(1)} %pad_maximum_fusion.mine), channel_id=1, source_target_pairs={{0,8},{8,0},{1,9},{9,1},{2,10},{10,2},{3,11},{11,3},{4,12},{12,4},... | collective-permute-start | bytes 5308424 | tf_op jit(solution)/shard_map/ppermute | solution.py:324
  96.7 5.5 %copy-start.16 = (f32[18,128]{1,0:T(8,128)S(1)}, f32[18,128]{1,0:T(8,128)}, u32[]{:S(2)}) copy-start(f32[18,128]{1,0:T(8,128)} %constant.71.clone) | copy-start | bytes 27652
  96.7 5.5 %copy-start.17 = (f32[18,128]{1,0:T(8,128)S(1)}, f32[18,128]{1,0:T(8,128)}, u32[]{:S(2)}) copy-start(f32[18,128]{1,0:T(8,128)} %constant.69.clone) | copy-start | bytes 27652
  96.7 5.5 %copy-start.9 = (f32[64,128]{1,0:T(8,128)S(1)}, f32[64,128]{1,0:T(8,128)}, u32[]{:S(2)}) copy-start(f32[64,128]{1,0:T(8,128)} %constant.80.clone) | copy-start | bytes 98308
  96.8 5.5 %copy-start.10 = (f32[64,128]{1,0:T(8,128)S(1)}, f32[64,128]{1,0:T(8,128)}, u32[]{:S(2)}) copy-start(f32[64,128]{1,0:T(8,128)} %constant.78.clone) | copy-start | bytes 98308
  96.8 5.5 %copy-start.11 = (f32[64,128]{1,0:T(8,128)S(1)}, f32[64,128]{1,0:T(8,128)}, u32[]{:S(2)}) copy-start(f32[64,128]{1,0:T(8,128)} %constant.79.clone) | copy-start | bytes 98308
  96.8 5.5 %copy-start.12 = (f32[64,128]{1,0:T(8,128)S(1)}, f32[64,128]{1,0:T(8,128)}, u32[]{:S(2)}) copy-start(f32[64,128]{1,0:T(8,128)} %constant.77.clone) | copy-start | bytes 98308
  96.8 5.5 %copy-start.13 = (f32[64,128]{1,0:T(8,128)S(1)}, f32[64,128]{1,0:T(8,128)}, u32[]{:S(2)}) copy-start(f32[64,128]{1,0:T(8,128)} %constant.75.clone) | copy-start | bytes 98308
  96.8 5.8 %copy-start.7 = (bf16[16,66,48]{2,1,0:T(8,128)(2,1)S(1)}, bf16[16,66,48]{2,1,0:T(8,128)(2,1)}, u32[]{:S(2)}) copy-start(bf16[16,66,48]{2,1,0:T(8,128)(2,1)} %pad_maximum_fusion.3) | copy-start | bytes 304132
  96.8 31.1 %all-to-all-start = ((bf16[32,112,256]{2,1,0:T(8,128)(2,1)}), bf16[32,112,256]{2,1,0:T(8,128)(2,1)}, u32[]{:S(2)}, u32[]{:S(2)}) async-start(bf16[32,112,256]{2,1,0:T(8,128)(2,1)} %branches.1), calls=%async_computation | async-start | bytes 3670016 | tf_op jit(solution)/shard_map/all_to_all | solution.py:348
  102.3 5.6 %copy-start.6 = (bf16[1280,256]{1,0:T(8,128)(2,1)S(1)}, bf16[1280,256]{1,0:T(8,128)(2,1)}, u32[]{:S(2)}) copy-start(bf16[1280,256]{1,0:T(8,128)(2,1)} %param.32) | copy-start | bytes 1966084
  102.6 23.5 %collective-permute-start.7 = (bf16[1,66,48]{2,1,0:T(8,128)(2,1)S(1)}, bf16[1,66,48]{2,1,0:T(8,128)(2,1)S(1)}, u32[]{:S(2)}, u32[]{:S(2)}) collective-permute-start(bf16[1,66,48]{2,1,0:T(8,128)(2,1)S(1)} %get-tuple-element.20), channel_id=1, source_target_pairs={{0,8},{8,16},{16,24},{24,32},{32,40},{40,48},{48,56},{56,64},{64,7... | collective-permute-start | bytes 19016 | tf_op jit(solution)/shard_map/ppermute | solution.py:349
  109.6 17.6 %collective-permute-start.8 = (bf16[1,66,48]{2,1,0:T(8,128)(2,1)S(1)}, bf16[1,66,48]{2,1,0:T(8,128)(2,1)S(1)}, u32[]{:S(2)}, u32[]{:S(2)}) collective-permute-start(bf16[1,66,48]{2,1,0:T(8,128)(2,1)S(1)} %get-tuple-element.19), channel_id=1, source_target_pairs={{8,0},{16,8},{24,16},{32,24},{40,32},{48,40},{56,48},{64,56},{72,6... | collective-permute-start | bytes 19016 | tf_op jit(solution)/shard_map/ppermute | solution.py:350
  (7 other events, 26.8 us)

commit v3 on v2

--- a/solution.py
+++ b/solution.py
@@ -110,17 +110,17 @@
     pick_one = own.astype(F32).astype(BF)
 
     def chunk(step, carry):
-        first = 6 * step
-        centre = x[pl.ds(first + 18, 6)].reshape(768, 256)
+        first = 9 * step
+        centre = x[pl.ds(first + 18, 9)].reshape(1152, 256)
         total = dot(dot(centre, w_one[...]).astype(BF), pick_one)
         for level in range(3):
             spacing = RATE * (level + 1)
-            upper = x[pl.ds(first + 18 - spacing, 6)].reshape(768, 256)
-            lower = x[pl.ds(first + 18 + spacing, 6)].reshape(768, 256)
+            upper = x[pl.ds(first + 18 - spacing, 9)].reshape(1152, 256)
+            lower = x[pl.ds(first + 18 + spacing, 9)].reshape(1152, 256)
             value = dot_t(centre, rhs[3 * level])
             value += dot_t(upper, rhs[3 * level + 1])
             value += dot_t(lower, rhs[3 * level + 2])
-            value = value.reshape(6, 128, 256)
+            value = value.reshape(9, 128, 256)
             from_left = ((lane_slot == 0) | (lane_slot == 3)) & (column >= spacing)
             from_right = (lane_slot == 2) & (column < 128 - spacing)
             moved = jnp.where(
@@ -131,36 +131,33 @@
                     value,
                     jnp.where(from_right, pltpu.roll(value, 128 - spacing, 1), 0.0),
                 ),
-            ).reshape(768, 256)
+            ).reshape(1152, 256)
             total += dot(moved.astype(BF), picks[level])
-        wide[pl.ds(first, 6), 8:136, :] = total.reshape(6, 128, 256)
+        wide[pl.ds(first, 9), 8:136, :] = total.reshape(9, 128, 256)
         return carry
 
-    lax.fori_loop(0, 3, chunk, 0)
-
-    def put(slot, index):
-        return pltpu.make_async_copy(ready.at[slot], out.at[index], out_sems.at[slot])
+    lax.fori_loop(0, 2, chunk, 0)
+
+    def put(index):
+        return pltpu.make_async_copy(ready.at[index], out.at[index], out_sems.at[index])
 
     def send(part, carry):
         for tile in range(8):
-            slot = tile % 2
             for line in range(6):
                 piece[18 * line : 18 * line + 18, :] = wide[
                     STRIP * part + line, 16 * tile + 7 : 16 * tile + 25, :
                 ]
-            if tile < 2:
-                @pl.when(part > 0)
-                def _():
-                    put(slot, 4 * (tile + 6) + part - 1).wait()
-            else:
-                put(slot, 4 * (tile - 2) + part).wait()
-            ready[slot] = piece[...].astype(BF)
-            put(slot, 4 * tile + part).start()
+            ready[4 * tile + part] = piece[...].astype(BF)
+            put(4 * tile + part).start()
         return carry
 
     lax.fori_loop(0, 4, send, 0)
-    put(0, 4 * 6 + 3).wait()
-    put(1, 4 * 7 + 3).wait()
+
+    def settle(index, carry):
+        put(index).wait()
+        return carry
+
+    lax.fori_loop(0, 32, settle, 0)
 
 
 def tail_kernel(
@@ -288,9 +285,6 @@
 
     across_y = lax.ppermute(features, "yh", swap())
 
-    low_flat = low_features.reshape(-1, low_features.shape[2])
-    low_mapped = jax.nn.relu(jnp.dot(low_flat, w_low, preferred_element_type=F32) + b_low)
-    low_mapped = low_mapped.astype(BF).reshape(16, 64, 48)
     taps = jnp.transpose(w_rate, (0, 1, 3, 2)).reshape(108, 256)
     unit = jnp.dot(jnp.asarray(tap_order(), BF), taps, preferred_element_type=F32)
     high, mid, rest = halves(jnp.sum(features, axis=(0, 1), dtype=F32)[None])
@@ -300,7 +294,10 @@
     unit = unit.astype(BF)[None]
 
     packed = lax.all_gather(unit, "z", axis=0, tiled=True)
-    across_y, packed, low_mapped = lax.optimization_barrier((across_y, packed, low_mapped))
+    across_y, packed, low_features = lax.optimization_barrier((across_y, packed, low_features))
+    low_flat = low_features.reshape(-1, low_features.shape[2])
+    low_mapped = jax.nn.relu(jnp.dot(low_flat, w_low, preferred_element_type=F32) + b_low)
+    low_mapped = low_mapped.astype(BF).reshape(16, 64, 48)
     eight = jnp.where(
         yh == 0,
         jnp.concatenate([features, across_y], axis=0),
@@ -338,9 +335,9 @@
             pltpu.VMEM((9, 256, 256), BF),
             pltpu.VMEM((EXT, 144, 256), F32),
             pltpu.VMEM((PIECE, 256), F32),
-            pltpu.VMEM((2, PIECE, 256), BF),
+            pltpu.VMEM((32, PIECE, 256), BF),
             pltpu.SemaphoreType.DMA((14,)),
-            pltpu.SemaphoreType.DMA((2,)),
+            pltpu.SemaphoreType.DMA((32,)),
         ],
         compiler_params=pltpu.CompilerParams(vmem_limit_bytes=28 << 20),
     )(place, joint, traded, packed, w_one, w_pool)

time: 135 us -> 128 us (0.948)
  Pallas kernels: 26.2 us -> 17.6 us
  other arithmetic: 3.88 us -> 5.35 us
  local copies, waits for them, and re-layouts: 3.05 us -> 4.49 us
    pallas_call x1, Pallas kernels: 20 us -> 11.4 us  [on_device(): pl.pallas_call(conv_kernel, name='branches', out_shape=jax.ShapeDtypeStru...]
    concatenate x1, other arithmetic: 0.24 us -> 1.71 us  [on_device(): joint = jnp.concatenate([eight, above, below, far], axis=0)]
    unnamed x40 -> x50, local copies, waits for them, and re-layouts: 0.16 us -> 1.6 us
where the time goes in v3:
time: 128 us; the launch traced here: 127 us
  starting transfers between devices  43.8 us (34%)
  blocking collectives  34.5 us (27%)
  waiting for transfers between devices  19 us (15%)
  Pallas kernels  17.6 us (14%)
  other arithmetic  5.35 us (4%)
  local copies, waits for them, and re-layouts  4.49 us (4%)
    all_gather x1, blocking collectives, on_device(): packed = lax.all_gather(unit, 'z', axis=0, tiled=True)  34.5 us
    ppermute x1, waiting for transfers between devices, on_device(): top = lax.ppermute(low_mapped[15:], ROWS, shift_pairs(row_count, 1))  14.5 us
    ppermute x1, starting transfers between devices, on_device(): traded = lax.ppermute(joint, 'core', swap())  13.3 us
    pallas_call x1, Pallas kernels, on_device(): pl.pallas_call(conv_kernel, name='branches', out_shape=jax.ShapeDtypeStru...  11.4 us
    pallas_call x1, Pallas kernels, on_device(): pl.pallas_call(tail_kernel, name='decoder', out_shape=(jax.ShapeDtypeStru...  6.2 us
    ppermute x1, starting transfers between devices, on_device(): across_y = lax.ppermute(features, 'yh', swap())  5.77 us
    all_to_all x1, starting transfers between devices, on_device(): received = lax.all_to_all(pieces, BLOCK, 0, 0, tiled=True)  5.18 us
    ppermute x1, starting transfers between devices, on_device(): top = lax.ppermute(low_mapped[15:], ROWS, shift_pairs(row_count, 1))  5.18 us
  transfers between devices with their start and end apart: 10, of which 4 were waited for; matrix products, arithmetic and copies ran while one was open for 6% of the time, Pallas kernels for 0%

profile of v3, /device:TPU:1, one launch (start us, length us, event | category | flops | bytes accessed | tf_op | source)
XLA Modules:
  0.0 127.1 jit_solution(14730145118610095571)
XLA Ops:
  0.7 5.8 %collective-permute-start = (bf16[4,128,256]{2,1,0:T(8,128)(2,1)}, bf16[4,128,256]{2,1,0:T(8,128)(2,1)S(1)}, u32[]{:S(2)}, u32[]{:S(2)}) collective-permute-start(bf16[4,128,256]{2,1,0:T(8,128)(2,1)} %param.26), channel_id=1, source_target_pairs={{0,16},{16,0},{1,17},{17,1},{2,18},{18,2},{3,19},{19,3},{4,20},{20... | collective-permute-start | bytes 786440 | tf_op jit(solution)/shard_map/ppermute | solution.py:286
  6.4 1.0 convert_reduce_fusion
  7.5 0.8 reshape.125
  8.4 0.9 fusion.4
  9.3 34.5 %all-gather = bf16[1792,256]{1,0:T(8,128)(2,1)S(1)} all-gather(bf16[112,256]{1,0:T(8,128)(2,1)S(1)} %fusion.4), channel_id=2, replica_groups=mesh['z'=16,'yh'=2,'core'=2,'x'=4,'yl'=2] {'z'}, dimensions={0}, use_global_device_ids=true | all-gather | bytes 974848 | tf_op jit(solution)/shard_map/all_gather | solution.py:296
  43.9 1.3 %collective-permute-start.1 = (bf16[8,128,256]{2,1,0:T(8,128)(2,1)S(1)}, bf16[8,128,256]{2,1,0:T(8,128)(2,1)S(1)}, u32[]{:S(2)}, u32[]{:S(2)}) collective-permute-start(bf16[8,128,256]{2,1,0:T(8,128)(2,1)S(1)} %maximum_select_fusion), channel_id=1, source_target_pairs={{0,32},{32,64},{64,96},{96,128},{128,160},{160,192},{192,224},{224... | collective-permute-start | bytes 1572872 | tf_op jit(solution)/shard_map/ppermute | solution.py:311
  45.2 1.3 %collective-permute-start.2 = (bf16[8,128,256]{2,1,0:T(8,128)(2,1)S(1)}, bf16[8,128,256]{2,1,0:T(8,128)(2,1)}, u32[]{:S(2)}, u32[]{:S(2)}) collective-permute-start(bf16[8,128,256]{2,1,0:T(8,128)(2,1)S(1)} %maximum_select_fusion), channel_id=1, source_target_pairs={{32,0},{64,32},{96,64},{128,96},{160,128},{192,160},{224,192},{256... | collective-permute-start | bytes 1572872 | tf_op jit(solution)/shard_map/ppermute | solution.py:312
  46.6 4.6 %collective-permute-start.3 = (bf16[3,128,256]{2,1,0:T(8,128)(2,1)S(1)}, bf16[3,128,256]{2,1,0:T(8,128)(2,1)S(1)}, u32[]{:S(2)}, u32[]{:S(2)}) collective-permute-start(bf16[3,128,256]{2,1,0:T(8,128)(2,1)S(1)} %select_select_fusion), channel_id=1, source_target_pairs={{8,72},{40,104},{72,136},{104,168},{136,200},{168,232},{200,264},{... | collective-permute-start | bytes 589832 | tf_op jit(solution)/shard_map/ppermute | solution.py:315
  51.6 1.3 %collective-permute-start.5 = (bf16[16,1,48]{2,1,0:T(2,128)(2,1)S(1)}, bf16[16,1,48]{2,1,0:T(2,128)(2,1)S(1)}, u32[]{:S(2)}, u32[]{:S(2)}) collective-permute-start(bf16[16,1,48]{2,1,0:T(2,128)(2,1)S(1)} %get-tuple-element.22), channel_id=1, source_target_pairs={{1,0},{2,1},{3,2},{4,3},{5,4},{6,5},{7,6},{9,8},{10,9},{11,10},{12... | collective-permute-start | bytes 4616 | tf_op jit(solution)/shard_map/ppermute | solution.py:317
  53.0 4.0 %collective-permute-start.4 = (bf16[16,1,48]{2,1,0:T(2,128)(2,1)S(1)}, bf16[16,1,48]{2,1,0:T(2,128)(2,1)S(1)}, u32[]{:S(2)}, u32[]{:S(2)}) collective-permute-start(bf16[16,1,48]{2,1,0:T(2,128)(2,1)S(1)} %get-tuple-element.21), channel_id=1, source_target_pairs={{0,1},{1,2},{2,3},{3,4},{4,5},{5,6},{6,7},{8,9},{9,10},{10,11},{11... | collective-permute-start | bytes 4616 | tf_op jit(solution)/shard_map/ppermute | solution.py:316
  57.7 0.8 pad_maximum_fusion.3
  59.2 0.8 copy-done.9
  60.0 1.7 %pad_maximum_fusion.mine = bf16[27,128,256]{2,1,0:T(8,128)(2,1)S(1)} fusion(bf16[3,128,256]{2,1,0:T(8,128)(2,1)} %copy-done.10, bf16[8,128,256]{2,1,0:T(8,128)(2,1)} %collective-permute-done.2, bf16[8,128,256]{2,1,0:T(8,128)(2,1)} %copy-done.9, bf16[8,128,256]{2,1,0:T(8,128)(2,1)} %copy-done.6), kind=kLoop, calls=%fused_computation | loop fusion | flops 2654208 | bytes 3538944 | tf_op jit(solution)/shard_map/concatenate | solution.py:320
  61.7 13.3 %collective-permute-start.6 = (bf16[27,128,256]{2,1,0:T(8,128)(2,1)S(1)}, bf16[27,128,256]{2,1,0:T(8,128)(2,1)}, u32[]{:S(2)}, u32[]{:S(2)}) collective-permute-start(bf16[27,128,256]{2,1,0:T(8,128)(2,1)S(1)} %pad_maximum_fusion.mine), channel_id=1, source_target_pairs={{0,8},{8,0},{1,9},{9,1},{2,10},{10,2},{3,11},{11,3},{4,12},{12,4},... | collective-permute-start | bytes 5308424 | tf_op jit(solution)/shard_map/ppermute | solution.py:321
  75.1 0.8 select_select_fusion.3
  75.9 2.6 %collective-permute-done.6.theirs = bf16[27,128,256]{2,1,0:T(8,128)(2,1)} collective-permute-done((bf16[27,128,256]{2,1,0:T(8,128)(2,1)S(1)}, bf16[27,128,256]{2,1,0:T(8,128)(2,1)}, u32[]{:S(2)}, u32[]{:S(2)}) %collective-permute-start.6) | collective-permute-done | bytes 1769504 | tf_op jit(solution)/shard_map/ppermute | solution.py:321
  78.4 11.4 %branches.1 = bf16[32,112,256]{2,1,0:T(8,128)(2,1)} custom-call(s32[2]{0:T(128)S(1)} %pad_add_fusion.place, bf16[27,128,256]{2,1,0:T(8,128)(2,1)S(1)} %pad_maximum_fusion.mine, bf16[27,128,256]{2,1,0:T(8,128)(2,1)} %collective-permute-done.6.theirs, bf16[16,112,256]{2,1,0:T(8,128)(2,1)S(1)} %bitcast.23, bf16[256,256]{1,0:T(8,128)(2,1)S(1)} %copy-done.1, ...), custom_call_target="tpu_custom_call" | custom-call | tf_op jit(solution)/shard_map/branches/pallas_call | solution.py:327
  89.9 5.2 %all-to-all-start = ((bf16[32,112,256]{2,1,0:T(8,128)(2,1)}), bf16[32,112,256]{2,1,0:T(8,128)(2,1)}, u32[]{:S(2)}, u32[]{:S(2)}) async-start(bf16[32,112,256]{2,1,0:T(8,128)(2,1)} %branches.1), calls=%async_computation | async-start | bytes 3670016 | tf_op jit(solution)/shard_map/all_to_all | solution.py:345
  95.5 5.2 %collective-permute-start.7 = (bf16[1,66,48]{2,1,0:T(8,128)(2,1)S(1)}, bf16[1,66,48]{2,1,0:T(8,128)(2,1)S(1)}, u32[]{:S(2)}, u32[]{:S(2)}) collective-permute-start(bf16[1,66,48]{2,1,0:T(8,128)(2,1)S(1)} %get-tuple-element.20), channel_id=1, source_target_pairs={{0,8},{8,16},{16,24},{24,32},{32,40},{40,48},{48,56},{56,64},{64,7... | collective-permute-start | bytes 19016 | tf_op jit(solution)/shard_map/ppermute | solution.py:346
  101.3 0.9 reshape.129.heads
  102.5 1.9 %collective-permute-start.8 = (bf16[1,66,48]{2,1,0:T(8,128)(2,1)S(1)}, bf16[1,66,48]{2,1,0:T(8,128)(2,1)S(1)}, u32[]{:S(2)}, u32[]{:S(2)}) collective-permute-start(bf16[1,66,48]{2,1,0:T(8,128)(2,1)S(1)} %get-tuple-element.19), channel_id=1, source_target_pairs={{8,0},{16,8},{24,16},{32,24},{40,32},{48,40},{56,48},{64,56},{72,6... | collective-permute-start | bytes 19016 | tf_op jit(solution)/shard_map/ppermute | solution.py:347
  104.5 14.5 %collective-permute-done.7 = bf16[1,66,48]{2,1,0:T(8,128)(2,1)S(1)} collective-permute-done((bf16[1,66,48]{2,1,0:T(8,128)(2,1)S(1)}, bf16[1,66,48]{2,1,0:T(8,128)(2,1)S(1)}, u32[]{:S(2)}, u32[]{:S(2)}) %collective-permute-start.7) | collective-permute-done | bytes 6368 | tf_op jit(solution)/shard_map/ppermute | solution.py:346
  119.1 1.1 collective-permute-done.8
  120.9 6.2 %decoder.1 = (bf16[4,16,256]{2,1,0:T(8,128)(2,1)}, bf16[16,64,256]{2,1,0:T(8,128)(2,1)}) custom-call(bf16[32,112,256]{2,1,0:T(8,128)(2,1)} %all-to-all-done.received, bf16[4,256,256]{2,1,0:T(8,128)(2,1)} %reshape.129.heads, bf16[256,256]{1,0:T(8,128)(2,1)S(1)} %slice.52.w_head, f32[4,256]{1,0:T(4,128)S(1)} %reshape.131.b_branch, f32[1,256]{1,0:T(1,128)S(1)} %slice.54.b_pool, ...), custom_call_target="tpu_custom_call" | custom-call | tf_op jit(solution)/shard_map/decoder/pallas_call | solution.py:354
  (84 shorter events, 4.0 us)
Async XLA Ops:
  0.6 50.5 %copy-start = (bf16[16,64,256]{2,1,0:T(8,128)(2,1)S(1)}, bf16[16,64,256]{2,1,0:T(8,128)(2,1)}, u32[]{:S(2)}) copy-start(bf16[16,64,256]{2,1,0:T(8,128)(2,1)} %param.27) | copy-start | bytes 1572868
  0.6 43.2 %copy-start.5 = (bf16[4,128,256]{2,1,0:T(8,128)(2,1)S(1)}, bf16[4,128,256]{2,1,0:T(8,128)(2,1)}, u32[]{:S(2)}) copy-start(bf16[4,128,256]{2,1,0:T(8,128)(2,1)} %param.26) | copy-start | bytes 786436
  0.7 43.2 %collective-permute-start = (bf16[4,128,256]{2,1,0:T(8,128)(2,1)}, bf16[4,128,256]{2,1,0:T(8,128)(2,1)S(1)}, u32[]{:S(2)}, u32[]{:S(2)}) collective-permute-start(bf16[4,128,256]{2,1,0:T(8,128)(2,1)} %param.26), channel_id=1, source_target_pairs={{0,16},{16,0},{1,17},{17,1},{2,18},{18,2},{3,19},{19,3},{4,20},{20... | collective-permute-start | bytes 786440 | tf_op jit(solution)/shard_map/ppermute | solution.py:286
  7.5 43.7 %copy-start.18 = (bf16[256,48]{0,1:T(8,128)(2,1)S(1)}, bf16[256,48]{0,1:T(8,128)(2,1)}, u32[]{:S(2)}) copy-start(bf16[256,48]{0,1:T(8,128)(2,1)} %param.34) | copy-start | bytes 73732
  7.5 43.7 %copy-start.23 = (f32[48]{0:T(128)S(1)}, f32[48]{0:T(128)}, u32[]{:S(2)}) copy-start(f32[48]{0:T(128)} %param.35) | copy-start | bytes 580
  43.9 14.7 %copy-start.6 = (bf16[8,128,256]{2,1,0:T(8,128)(2,1)}, bf16[8,128,256]{2,1,0:T(8,128)(2,1)S(1)}, u32[]{:S(2)}) copy-start(bf16[8,128,256]{2,1,0:T(8,128)(2,1)S(1)} %maximum_select_fusion) | copy-start | bytes 1572868
  43.9 14.7 %collective-permute-start.1 = (bf16[8,128,256]{2,1,0:T(8,128)(2,1)S(1)}, bf16[8,128,256]{2,1,0:T(8,128)(2,1)S(1)}, u32[]{:S(2)}, u32[]{:S(2)}) collective-permute-start(bf16[8,128,256]{2,1,0:T(8,128)(2,1)S(1)} %maximum_select_fusion), channel_id=1, source_target_pairs={{0,32},{32,64},{64,96},{96,128},{128,160},{160,192},{192,224},{224... | collective-permute-start | bytes 1572872 | tf_op jit(solution)/shard_map/ppermute | solution.py:311
  45.2 14.8 %collective-permute-start.2 = (bf16[8,128,256]{2,1,0:T(8,128)(2,1)S(1)}, bf16[8,128,256]{2,1,0:T(8,128)(2,1)}, u32[]{:S(2)}, u32[]{:S(2)}) collective-permute-start(bf16[8,128,256]{2,1,0:T(8,128)(2,1)S(1)} %maximum_select_fusion), channel_id=1, source_target_pairs={{32,0},{64,32},{96,64},{128,96},{160,128},{192,160},{224,192},{256... | collective-permute-start | bytes 1572872 | tf_op jit(solution)/shard_map/ppermute | solution.py:312
  46.6 12.0 %collective-permute-start.3 = (bf16[3,128,256]{2,1,0:T(8,128)(2,1)S(1)}, bf16[3,128,256]{2,1,0:T(8,128)(2,1)S(1)}, u32[]{:S(2)}, u32[]{:S(2)}) collective-permute-start(bf16[3,128,256]{2,1,0:T(8,128)(2,1)S(1)} %select_select_fusion), channel_id=1, source_target_pairs={{8,72},{40,104},{72,136},{104,168},{136,200},{168,232},{200,264},{... | collective-permute-start | bytes 589832 | tf_op jit(solution)/shard_map/ppermute | solution.py:315
  51.6 5.3 %collective-permute-start.5 = (bf16[16,1,48]{2,1,0:T(2,128)(2,1)S(1)}, bf16[16,1,48]{2,1,0:T(2,128)(2,1)S(1)}, u32[]{:S(2)}, u32[]{:S(2)}) collective-permute-start(bf16[16,1,48]{2,1,0:T(2,128)(2,1)S(1)} %get-tuple-element.22), channel_id=1, source_target_pairs={{1,0},{2,1},{3,2},{4,3},{5,4},{6,5},{7,6},{9,8},{10,9},{11,10},{12... | collective-permute-start | bytes 4616 | tf_op jit(solution)/shard_map/ppermute | solution.py:317
  53.0 4.8 %collective-permute-start.4 = (bf16[16,1,48]{2,1,0:T(2,128)(2,1)S(1)}, bf16[16,1,48]{2,1,0:T(2,128)(2,1)S(1)}, u32[]{:S(2)}, u32[]{:S(2)}) collective-permute-start(bf16[16,1,48]{2,1,0:T(2,128)(2,1)S(1)} %get-tuple-element.21), channel_id=1, source_target_pairs={{0,1},{1,2},{2,3},{3,4},{4,5},{5,6},{6,7},{8,9},{9,10},{10,11},{11... | collective-permute-start | bytes 4616 | tf_op jit(solution)/shard_map/ppermute | solution.py:316
  58.5 16.6 %copy-start.11 = (f32[64,128]{1,0:T(8,128)S(1)}, f32[64,128]{1,0:T(8,128)}, u32[]{:S(2)}) copy-start(f32[64,128]{1,0:T(8,128)} %constant.74.clone) | copy-start | bytes 98308
  58.5 19.9 %copy-start.1 = (bf16[256,256]{1,0:T(8,128)(2,1)S(1)}, bf16[256,256]{1,0:T(8,128)(2,1)}, u32[]{:S(2)}) copy-start(bf16[256,256]{1,0:T(8,128)(2,1)} %w_one.1) | copy-start | bytes 393220
  58.5 19.9 %copy-start.2 = (bf16[256,256]{1,0:T(8,128)(2,1)S(1)}, bf16[256,256]{1,0:T(8,128)(2,1)}, u32[]{:S(2)}) copy-start(bf16[256,256]{1,0:T(8,128)(2,1)} %w_pool.1) | copy-start | bytes 393220
  61.7 16.7 %collective-permute-start.6 = (bf16[27,128,256]{2,1,0:T(8,128)(2,1)S(1)}, bf16[27,128,256]{2,1,0:T(8,128)(2,1)}, u32[]{:S(2)}, u32[]{:S(2)}) collective-permute-start(bf16[27,128,256]{2,1,0:T(8,128)(2,1)S(1)} %pad_maximum_fusion.mine), channel_id=1, source_target_pairs={{0,8},{8,0},{1,9},{9,1},{2,10},{10,2},{3,11},{11,3},{4,12},{12,4},... | collective-permute-start | bytes 5308424 | tf_op jit(solution)/shard_map/ppermute | solution.py:321
  89.8 5.3 %copy-start.12 = (f32[64,128]{1,0:T(8,128)S(1)}, f32[64,128]{1,0:T(8,128)}, u32[]{:S(2)}) copy-start(f32[64,128]{1,0:T(8,128)} %constant.80.clone) | copy-start | bytes 98308
  89.8 5.3 %copy-start.13 = (f32[64,128]{1,0:T(8,128)S(1)}, f32[64,128]{1,0:T(8,128)}, u32[]{:S(2)}) copy-start(f32[64,128]{1,0:T(8,128)} %constant.78.clone) | copy-start | bytes 98308
  89.9 5.6 %copy-start.8 = (bf16[16,66,48]{2,1,0:T(8,128)(2,1)S(1)}, bf16[16,66,48]{2,1,0:T(8,128)(2,1)}, u32[]{:S(2)}) copy-start(bf16[16,66,48]{2,1,0:T(8,128)(2,1)} %pad_maximum_fusion.3) | copy-start | bytes 304132
  89.9 31.0 %all-to-all-start = ((bf16[32,112,256]{2,1,0:T(8,128)(2,1)}), bf16[32,112,256]{2,1,0:T(8,128)(2,1)}, u32[]{:S(2)}, u32[]{:S(2)}) async-start(bf16[32,112,256]{2,1,0:T(8,128)(2,1)} %branches.1), calls=%async_computation | async-start | bytes 3670016 | tf_op jit(solution)/shard_map/all_to_all | solution.py:345
  95.2 5.6 %copy-start.7 = (bf16[1280,256]{1,0:T(8,128)(2,1)S(1)}, bf16[1280,256]{1,0:T(8,128)(2,1)}, u32[]{:S(2)}) copy-start(bf16[1280,256]{1,0:T(8,128)(2,1)} %param.32) | copy-start | bytes 1966084
  95.5 5.4 %copy-start.19 = (f32[5,256]{1,0:T(8,128)S(1)}, f32[5,256]{1,0:T(8,128)}, u32[]{:S(2)}) copy-start(f32[5,256]{1,0:T(8,128)} %param.31) | copy-start | bytes 15364
  95.5 5.4 %slice-start = ((bf16[1280,256]{1,0:T(8,128)(2,1)}), bf16[1024,256]{1,0:T(8,128)(2,1)S(1)}, s32[]{:S(2)}) async-start(bf16[1280,256]{1,0:T(8,128)(2,1)} %param.32), calls=%async_computation.1 | async-start | bytes 1048576 | tf_op jit(solution)/shard_map/slice | solution.py:351
  95.5 23.5 %collective-permute-start.7 = (bf16[1,66,48]{2,1,0:T(8,128)(2,1)S(1)}, bf16[1,66,48]{2,1,0:T(8,128)(2,1)S(1)}, u32[]{:S(2)}, u32[]{:S(2)}) collective-permute-start(bf16[1,66,48]{2,1,0:T(8,128)(2,1)S(1)} %get-tuple-element.20), channel_id=1, source_target_pairs={{0,8},{8,16},{16,24},{24,32},{32,40},{40,48},{48,56},{56,64},{64,7... | collective-permute-start | bytes 19016 | tf_op jit(solution)/shard_map/ppermute | solution.py:346
  102.5 17.6 %collective-permute-start.8 = (bf16[1,66,48]{2,1,0:T(8,128)(2,1)S(1)}, bf16[1,66,48]{2,1,0:T(8,128)(2,1)S(1)}, u32[]{:S(2)}, u32[]{:S(2)}) collective-permute-start(bf16[1,66,48]{2,1,0:T(8,128)(2,1)S(1)} %get-tuple-element.19), channel_id=1, source_target_pairs={{8,0},{16,8},{24,16},{32,24},{40,32},{48,40},{56,48},{64,56},{72,6... | collective-permute-start | bytes 19016 | tf_op jit(solution)/shard_map/ppermute | solution.py:347
  (12 other events, 43.7 us)

commit v4 on v3

--- a/solution.py
+++ b/solution.py
@@ -158,6 +158,11 @@
         return carry
 
     lax.fori_loop(0, 32, settle, 0)
+
+
+def low_kernel(low_features, w_low, b_low, out):
+    value = dot(low_features[...], w_low[...]) + b_low[...]
+    out[...] = jnp.maximum(value, 0.0).astype(BF)
 
 
 def tail_kernel(
@@ -296,8 +301,14 @@
     packed = lax.all_gather(unit, "z", axis=0, tiled=True)
     across_y, packed, low_features = lax.optimization_barrier((across_y, packed, low_features))
     low_flat = low_features.reshape(-1, low_features.shape[2])
-    low_mapped = jax.nn.relu(jnp.dot(low_flat, w_low, preferred_element_type=F32) + b_low)
-    low_mapped = low_mapped.astype(BF).reshape(16, 64, 48)
+    low_mapped = pl.pallas_call(
+        low_kernel,
+        name="low",
+        out_shape=jax.ShapeDtypeStruct((1024, 48), BF),
+        in_specs=[pl.BlockSpec(memory_space=pltpu.VMEM)] * 3,
+        out_specs=pl.BlockSpec(memory_space=pltpu.VMEM),
+        compiler_params=pltpu.CompilerParams(vmem_limit_bytes=4 << 20),
+    )(low_flat, w_low, b_low[None]).reshape(16, 64, 48)
     eight = jnp.where(
         yh == 0,
         jnp.concatenate([features, across_y], axis=0),
@@ -339,7 +350,7 @@
             pltpu.SemaphoreType.DMA((14,)),
             pltpu.SemaphoreType.DMA((32,)),
         ],
-        compiler_params=pltpu.CompilerParams(vmem_limit_bytes=28 << 20),
+        compiler_params=pltpu.CompilerParams(vmem_limit_bytes=52 << 20),
     )(place, joint, traded, packed, w_one, w_pool)
     pieces = held(pieces)
     received = lax.all_to_all(pieces, BLOCK, 0, 0, tiled=True)
@@ -371,7 +382,7 @@
         ],
         compiler_params=pltpu.CompilerParams(vmem_limit_bytes=20 << 20),
     )(
-        received,
+        pltpu.with_memory_space_constraint(received, pltpu.VMEM),
         held(heads),
         w_proj[1024:],
         biases,

time: 128 us -> 125 us (0.977)
  other arithmetic: 5.35 us -> 2.42 us
  local copies, waits for them, and re-layouts: 4.49 us -> 6.63 us
  waiting for transfers between devices: 19 us -> 17.1 us
    reshape x3, local copies, waits for them, and re-layouts: 1.29 us -> 3.12 us  [on_device(): w_proj[:1024].reshape(4, 16, 4, 4, 256).transpose(2, 0, 1, 3, 4)]
    ppermute x1, waiting for transfers between devices: 14.5 us -> 12.9 us  [on_device(): top = lax.ppermute(low_mapped[15:], ROWS, shift_pairs(row_count, 1))]
    pallas_call x1, Pallas kernels: 6.2 us -> 4.7 us  [on_device(): pl.pallas_call(tail_kernel, name='decoder', out_shape=(jax.ShapeDtypeStru...]
    concatenate x1, other arithmetic: 1.71 us -> 0.24 us  [on_device(): joint = jnp.concatenate([eight, above, below, far], axis=0)]
  transfers between devices with their start and end apart: 10 -> 10, of which waited for: 4 -> 4; matrix products, arithmetic and copies ran while one was open for 6% -> 8% of each run, Pallas kernels for 0% -> 0%
where the time goes in v4:
time: 125 us; the launch traced here: 124 us
  starting transfers between devices  44.4 us (36%)
  blocking collectives  34.5 us (28%)
  waiting for transfers between devices  17.1 us (14%)
  Pallas kernels  16.9 us (14%)
  local copies, waits for them, and re-layouts  6.63 us (5%)
  other arithmetic  2.42 us (2%)
  between operations  1.27 us (1%)
    all_gather x1, blocking collectives, on_device(): packed = lax.all_gather(unit, 'z', axis=0, tiled=True)  34.5 us
    ppermute x1, starting transfers between devices, on_device(): traded = lax.ppermute(joint, 'core', swap())  14 us
    ppermute x1, waiting for transfers between devices, on_device(): top = lax.ppermute(low_mapped[15:], ROWS, shift_pairs(row_count, 1))  12.9 us
    pallas_call x1, Pallas kernels, on_device(): pl.pallas_call(conv_kernel, name='branches', out_shape=jax.ShapeDtypeStru...  11.9 us
    ppermute x1, starting transfers between devices, on_device(): across_y = lax.ppermute(features, 'yh', swap())  5.77 us
    all_to_all x1, starting transfers between devices, on_device(): received = lax.all_to_all(pieces, BLOCK, 0, 0, tiled=True)  5.14 us
    ppermute x1, starting transfers between devices, on_device(): top = lax.ppermute(low_mapped[15:], ROWS, shift_pairs(row_count, 1))  5.04 us
    pallas_call x1, Pallas kernels, on_device(): pl.pallas_call(tail_kernel, name='decoder', out_shape=(jax.ShapeDtypeStru...  4.7 us
  transfers between devices with their start and end apart: 10, of which 4 were waited for; matrix products, arithmetic and copies ran while one was open for 8% of the time, Pallas kernels for 0%

profile of v4, /device:TPU:1, one launch (start us, length us, event | category | flops | bytes accessed | tf_op | source)
XLA Modules:
  0.0 124.1 jit_solution(2155687072841897595)
XLA Ops:
  0.6 5.8 %collective-permute-start = (bf16[4,128,256]{2,1,0:T(8,128)(2,1)}, bf16[4,128,256]{2,1,0:T(8,128)(2,1)S(1)}, u32[]{:S(2)}, u32[]{:S(2)}) collective-permute-start(bf16[4,128,256]{2,1,0:T(8,128)(2,1)} %param.26), channel_id=1, source_target_pairs={{0,16},{16,0},{1,17},{17,1},{2,18},{18,2},{3,19},{19,3},{4,20},{20... | collective-permute-start | bytes 786440 | tf_op jit(solution)/shard_map/ppermute | solution.py:291
  6.4 1.0 convert_reduce_fusion
  7.5 0.9 reshape.124
  8.4 0.9 copy.31.w_low
  9.3 0.9 fusion.2
  10.2 34.5 %all-gather = bf16[1792,256]{1,0:T(8,128)(2,1)S(1)} all-gather(bf16[112,256]{1,0:T(8,128)(2,1)S(1)} %fusion.2), channel_id=2, replica_groups=mesh['z'=16,'yh'=2,'core'=2,'x'=4,'yl'=2] {'z'}, dimensions={0}, use_global_device_ids=true | all-gather | bytes 974848 | tf_op jit(solution)/shard_map/all_gather | solution.py:301
  44.8 1.3 %collective-permute-start.1 = (bf16[8,128,256]{2,1,0:T(8,128)(2,1)S(1)}, bf16[8,128,256]{2,1,0:T(8,128)(2,1)S(1)}, u32[]{:S(2)}, u32[]{:S(2)}) collective-permute-start(bf16[8,128,256]{2,1,0:T(8,128)(2,1)S(1)} %maximum_select_fusion), channel_id=1, source_target_pairs={{0,32},{32,64},{64,96},{96,128},{128,160},{160,192},{192,224},{224... | collective-permute-start | bytes 1572872 | tf_op jit(solution)/shard_map/ppermute | solution.py:322
  46.1 1.3 %collective-permute-start.2 = (bf16[8,128,256]{2,1,0:T(8,128)(2,1)S(1)}, bf16[8,128,256]{2,1,0:T(8,128)(2,1)S(1)}, u32[]{:S(2)}, u32[]{:S(2)}) collective-permute-start(bf16[8,128,256]{2,1,0:T(8,128)(2,1)S(1)} %maximum_select_fusion), channel_id=1, source_target_pairs={{32,0},{64,32},{96,64},{128,96},{160,128},{192,160},{224,192},{256... | collective-permute-start | bytes 1572872 | tf_op jit(solution)/shard_map/ppermute | solution.py:323
  47.5 4.6 %collective-permute-start.3 = (bf16[3,128,256]{2,1,0:T(8,128)(2,1)S(1)}, bf16[3,128,256]{2,1,0:T(8,128)(2,1)S(1)}, u32[]{:S(2)}, u32[]{:S(2)}) collective-permute-start(bf16[3,128,256]{2,1,0:T(8,128)(2,1)S(1)} %select_select_fusion), channel_id=1, source_target_pairs={{8,72},{40,104},{72,136},{104,168},{136,200},{168,232},{200,264},{... | collective-permute-start | bytes 589832 | tf_op jit(solution)/shard_map/ppermute | solution.py:326
  52.4 1.3 %collective-permute-start.5 = (bf16[16,1,48]{2,1,0:T(2,128)(2,1)S(1)}, bf16[16,1,48]{2,1,0:T(2,128)(2,1)S(1)}, u32[]{:S(2)}, u32[]{:S(2)}) collective-permute-start(bf16[16,1,48]{2,1,0:T(2,128)(2,1)S(1)} %get-tuple-element.22), channel_id=1, source_target_pairs={{1,0},{2,1},{3,2},{4,3},{5,4},{6,5},{7,6},{9,8},{10,9},{11,10},{12... | collective-permute-start | bytes 4616 | tf_op jit(solution)/shard_map/ppermute | solution.py:328
  53.7 4.0 %collective-permute-start.4 = (bf16[16,1,48]{2,1,0:T(2,128)(2,1)S(1)}, bf16[16,1,48]{2,1,0:T(2,128)(2,1)S(1)}, u32[]{:S(2)}, u32[]{:S(2)}) collective-permute-start(bf16[16,1,48]{2,1,0:T(2,128)(2,1)S(1)} %get-tuple-element.21), channel_id=1, source_target_pairs={{0,1},{1,2},{2,3},{3,4},{4,5},{5,6},{6,7},{8,9},{9,10},{10,11},{11... | collective-permute-start | bytes 4616 | tf_op jit(solution)/shard_map/ppermute | solution.py:327
  57.7 0.8 collective-permute-done.4
  58.9 14.0 %collective-permute-start.6 = (bf16[27,128,256]{2,1,0:T(8,128)(2,1)S(1)}, bf16[27,128,256]{2,1,0:T(8,128)(2,1)}, u32[]{:S(2)}, u32[]{:S(2)}) collective-permute-start(bf16[27,128,256]{2,1,0:T(8,128)(2,1)S(1)} %pad_maximum_fusion.mine), channel_id=1, source_target_pairs={{0,8},{8,0},{1,9},{9,1},{2,10},{10,2},{3,11},{11,3},{4,12},{12,4},... | collective-permute-start | bytes 5308424 | tf_op jit(solution)/shard_map/ppermute | solution.py:332
  73.1 3.3 %collective-permute-done.6.theirs = bf16[27,128,256]{2,1,0:T(8,128)(2,1)} collective-permute-done((bf16[27,128,256]{2,1,0:T(8,128)(2,1)S(1)}, bf16[27,128,256]{2,1,0:T(8,128)(2,1)}, u32[]{:S(2)}, u32[]{:S(2)}) %collective-permute-start.6) | collective-permute-done | bytes 1769504 | tf_op jit(solution)/shard_map/ppermute | solution.py:332
  76.4 11.9 %branches.1 = bf16[32,112,256]{2,1,0:T(8,128)(2,1)} custom-call(s32[2]{0:T(128)S(1)} %pad_add_fusion.place, bf16[27,128,256]{2,1,0:T(8,128)(2,1)} %copy-done.6, bf16[27,128,256]{2,1,0:T(8,128)(2,1)} %collective-permute-done.6.theirs, bf16[16,112,256]{2,1,0:T(8,128)(2,1)S(1)} %bitcast.21, bf16[256,256]{1,0:T(8,128)(2,1)S(1)} %copy-done.1, ...), custom_call_target="tpu_custom_call" | custom-call | tf_op jit(solution)/shard_map/branches/pallas_call | solution.py:338
  88.4 5.1 %all-to-all-start = ((bf16[32,112,256]{2,1,0:T(8,128)(2,1)}), bf16[32,112,256]{2,1,0:T(8,128)(2,1)S(1)}, u32[]{:S(2)}, u32[]{:S(2)}) async-start(bf16[32,112,256]{2,1,0:T(8,128)(2,1)} %branches.1), calls=%async_computation | async-start | bytes 3670016 | tf_op jit(solution)/shard_map/all_to_all | solution.py:356
  93.9 5.0 %collective-permute-start.7 = (bf16[1,66,48]{2,1,0:T(8,128)(2,1)S(1)}, bf16[1,66,48]{2,1,0:T(8,128)(2,1)S(1)}, u32[]{:S(2)}, u32[]{:S(2)}) collective-permute-start(bf16[1,66,48]{2,1,0:T(8,128)(2,1)S(1)} %get-tuple-element.20), channel_id=1, source_target_pairs={{0,8},{8,16},{16,24},{24,32},{32,40},{40,48},{48,56},{56,64},{64,7... | collective-permute-start | bytes 19016 | tf_op jit(solution)/shard_map/ppermute | solution.py:357
  99.2 0.9 reshape.127
  100.1 1.3 %copy.35 = bf16[4,16,4,4,256]{4,3,1,0,2:T(4,128)(2,1)S(1)} copy(bf16[4,16,4,4,256]{4,3,2,1,0:T(4,128)(2,1)} %reshape.127) | data formatting | bytes 1048576 | tf_op jit(solution)/shard_map/reshape | solution.py:362
  101.4 0.9 reshape.128.heads
  102.7 1.9 %collective-permute-start.8 = (bf16[1,66,48]{2,1,0:T(8,128)(2,1)S(1)}, bf16[1,66,48]{2,1,0:T(8,128)(2,1)S(1)}, u32[]{:S(2)}, u32[]{:S(2)}) collective-permute-start(bf16[1,66,48]{2,1,0:T(8,128)(2,1)S(1)} %get-tuple-element.19), channel_id=1, source_target_pairs={{8,0},{16,8},{24,16},{32,24},{40,32},{48,40},{56,48},{64,56},{72,6... | collective-permute-start | bytes 19016 | tf_op jit(solution)/shard_map/ppermute | solution.py:358
  104.6 12.9 %collective-permute-done.7 = bf16[1,66,48]{2,1,0:T(8,128)(2,1)S(1)} collective-permute-done((bf16[1,66,48]{2,1,0:T(8,128)(2,1)S(1)}, bf16[1,66,48]{2,1,0:T(8,128)(2,1)S(1)}, u32[]{:S(2)}, u32[]{:S(2)}) %collective-permute-start.7) | collective-permute-done | bytes 6368 | tf_op jit(solution)/shard_map/ppermute | solution.py:357
  117.6 1.0 constant_dynamic-update-slice_fusion.1
  119.4 4.7 %decoder.1 = (bf16[4,16,256]{2,1,0:T(8,128)(2,1)}, bf16[16,64,256]{2,1,0:T(8,128)(2,1)}) custom-call(bf16[32,112,256]{2,1,0:T(8,128)(2,1)S(1)} %all-to-all-done.received, bf16[4,256,256]{2,1,0:T(8,128)(2,1)} %reshape.128.heads, bf16[256,256]{1,0:T(8,128)(2,1)S(1)} %slice.52.w_head, f32[4,256]{1,0:T(4,128)S(1)} %reshape.130.b_branch, ...), custom_call_target="tpu_custom_call" | custom-call | tf_op jit(solution)/shard_map/decoder/pallas_call | solution.py:365
  (81 shorter events, 2.5 us)
Async XLA Ops:
  0.6 44.1 %copy-start.7 = (bf16[4,128,256]{2,1,0:T(8,128)(2,1)S(1)}, bf16[4,128,256]{2,1,0:T(8,128)(2,1)}, u32[]{:S(2)}) copy-start(bf16[4,128,256]{2,1,0:T(8,128)(2,1)} %param.26) | copy-start | bytes 786436
  0.6 44.1 %collective-permute-start = (bf16[4,128,256]{2,1,0:T(8,128)(2,1)}, bf16[4,128,256]{2,1,0:T(8,128)(2,1)S(1)}, u32[]{:S(2)}, u32[]{:S(2)}) collective-permute-start(bf16[4,128,256]{2,1,0:T(8,128)(2,1)} %param.26), channel_id=1, source_target_pairs={{0,16},{16,0},{1,17},{17,1},{2,18},{18,2},{3,19},{19,3},{4,20},{20... | collective-permute-start | bytes 786440 | tf_op jit(solution)/shard_map/ppermute | solution.py:291
  7.5 44.6 %copy-start = (bf16[16,64,256]{2,1,0:T(8,128)(2,1)S(1)}, bf16[16,64,256]{2,1,0:T(8,128)(2,1)}, u32[]{:S(2)}) copy-start(bf16[16,64,256]{2,1,0:T(8,128)(2,1)} %param.27) | copy-start | bytes 1572868
  7.5 44.6 %copy-start.5 = (f32[48]{0:T(128)S(1)}, f32[48]{0:T(128)}, u32[]{:S(2)}) copy-start(f32[48]{0:T(128)} %param.35) | copy-start | bytes 580
  44.8 13.9 %collective-permute-start.1 = (bf16[8,128,256]{2,1,0:T(8,128)(2,1)S(1)}, bf16[8,128,256]{2,1,0:T(8,128)(2,1)S(1)}, u32[]{:S(2)}, u32[]{:S(2)}) collective-permute-start(bf16[8,128,256]{2,1,0:T(8,128)(2,1)S(1)} %maximum_select_fusion), channel_id=1, source_target_pairs={{0,32},{32,64},{64,96},{96,128},{128,160},{160,192},{192,224},{224... | collective-permute-start | bytes 1572872 | tf_op jit(solution)/shard_map/ppermute | solution.py:322
  46.1 12.5 %collective-permute-start.2 = (bf16[8,128,256]{2,1,0:T(8,128)(2,1)S(1)}, bf16[8,128,256]{2,1,0:T(8,128)(2,1)S(1)}, u32[]{:S(2)}, u32[]{:S(2)}) collective-permute-start(bf16[8,128,256]{2,1,0:T(8,128)(2,1)S(1)} %maximum_select_fusion), channel_id=1, source_target_pairs={{32,0},{64,32},{96,64},{128,96},{160,128},{192,160},{224,192},{256... | collective-permute-start | bytes 1572872 | tf_op jit(solution)/shard_map/ppermute | solution.py:323
  47.5 11.2 %collective-permute-start.3 = (bf16[3,128,256]{2,1,0:T(8,128)(2,1)S(1)}, bf16[3,128,256]{2,1,0:T(8,128)(2,1)S(1)}, u32[]{:S(2)}, u32[]{:S(2)}) collective-permute-start(bf16[3,128,256]{2,1,0:T(8,128)(2,1)S(1)} %select_select_fusion), channel_id=1, source_target_pairs={{8,72},{40,104},{72,136},{104,168},{136,200},{168,232},{200,264},{... | collective-permute-start | bytes 589832 | tf_op jit(solution)/shard_map/ppermute | solution.py:326
  52.4 5.3 %collective-permute-start.5 = (bf16[16,1,48]{2,1,0:T(2,128)(2,1)S(1)}, bf16[16,1,48]{2,1,0:T(2,128)(2,1)S(1)}, u32[]{:S(2)}, u32[]{:S(2)}) collective-permute-start(bf16[16,1,48]{2,1,0:T(2,128)(2,1)S(1)} %get-tuple-element.22), channel_id=1, source_target_pairs={{1,0},{2,1},{3,2},{4,3},{5,4},{6,5},{7,6},{9,8},{10,9},{11,10},{12... | collective-permute-start | bytes 4616 | tf_op jit(solution)/shard_map/ppermute | solution.py:328
  53.7 4.8 %collective-permute-start.4 = (bf16[16,1,48]{2,1,0:T(2,128)(2,1)S(1)}, bf16[16,1,48]{2,1,0:T(2,128)(2,1)S(1)}, u32[]{:S(2)}, u32[]{:S(2)}) collective-permute-start(bf16[16,1,48]{2,1,0:T(2,128)(2,1)S(1)} %get-tuple-element.21), channel_id=1, source_target_pairs={{0,1},{1,2},{2,3},{3,4},{4,5},{5,6},{6,7},{8,9},{9,10},{10,11},{11... | collective-permute-start | bytes 4616 | tf_op jit(solution)/shard_map/ppermute | solution.py:327
  58.6 35.4 %copy-start.8 = (bf16[16,66,48]{2,1,0:T(8,128)(2,1)}, bf16[16,66,48]{2,1,0:T(8,128)(2,1)S(1)}, u32[]{:S(2)}) copy-start(bf16[16,66,48]{2,1,0:T(8,128)(2,1)S(1)} %pad_maximum_fusion.3) | copy-start | bytes 304132
  58.6 14.5 %copy-start.10 = (f32[64,128]{1,0:T(8,128)S(1)}, f32[64,128]{1,0:T(8,128)}, u32[]{:S(2)}) copy-start(f32[64,128]{1,0:T(8,128)} %constant.72.clone) | copy-start | bytes 98308
  58.6 14.5 %copy-start.11 = (f32[64,128]{1,0:T(8,128)S(1)}, f32[64,128]{1,0:T(8,128)}, u32[]{:S(2)}) copy-start(f32[64,128]{1,0:T(8,128)} %constant.70.clone) | copy-start | bytes 98308
  58.6 14.5 %copy-start.12 = (f32[64,128]{1,0:T(8,128)S(1)}, f32[64,128]{1,0:T(8,128)}, u32[]{:S(2)}) copy-start(f32[64,128]{1,0:T(8,128)} %constant.71.clone) | copy-start | bytes 98308
  58.6 17.8 %copy-start.1 = (bf16[256,256]{1,0:T(8,128)(2,1)S(1)}, bf16[256,256]{1,0:T(8,128)(2,1)}, u32[]{:S(2)}) copy-start(bf16[256,256]{1,0:T(8,128)(2,1)} %w_one.1) | copy-start | bytes 393220
  58.6 17.8 %copy-start.2 = (bf16[256,256]{1,0:T(8,128)(2,1)S(1)}, bf16[256,256]{1,0:T(8,128)(2,1)}, u32[]{:S(2)}) copy-start(bf16[256,256]{1,0:T(8,128)(2,1)} %w_pool.1) | copy-start | bytes 393220
  58.9 17.5 %copy-start.6 = (bf16[27,128,256]{2,1,0:T(8,128)(2,1)}, bf16[27,128,256]{2,1,0:T(8,128)(2,1)S(1)}, u32[]{:S(2)}) copy-start(bf16[27,128,256]{2,1,0:T(8,128)(2,1)S(1)} %pad_maximum_fusion.mine) | copy-start | bytes 5308420
  58.9 17.5 %collective-permute-start.6 = (bf16[27,128,256]{2,1,0:T(8,128)(2,1)S(1)}, bf16[27,128,256]{2,1,0:T(8,128)(2,1)}, u32[]{:S(2)}, u32[]{:S(2)}) collective-permute-start(bf16[27,128,256]{2,1,0:T(8,128)(2,1)S(1)} %pad_maximum_fusion.mine), channel_id=1, source_target_pairs={{0,8},{8,0},{1,9},{9,1},{2,10},{10,2},{3,11},{11,3},{4,12},{12,4},... | collective-permute-start | bytes 5308424 | tf_op jit(solution)/shard_map/ppermute | solution.py:332
  88.3 5.3 %copy-start.13 = (f32[64,128]{1,0:T(8,128)S(1)}, f32[64,128]{1,0:T(8,128)}, u32[]{:S(2)}) copy-start(f32[64,128]{1,0:T(8,128)} %constant.78.clone) | copy-start | bytes 98308
  88.3 5.3 %copy-start.14 = (f32[64,128]{1,0:T(8,128)S(1)}, f32[64,128]{1,0:T(8,128)}, u32[]{:S(2)}) copy-start(f32[64,128]{1,0:T(8,128)} %constant.76.clone) | copy-start | bytes 98308
  88.4 5.3 %copy-start.15 = (f32[64,128]{1,0:T(8,128)S(1)}, f32[64,128]{1,0:T(8,128)}, u32[]{:S(2)}) copy-start(f32[64,128]{1,0:T(8,128)} %constant.77.clone) | copy-start | bytes 98308
  88.4 31.0 %all-to-all-start = ((bf16[32,112,256]{2,1,0:T(8,128)(2,1)}), bf16[32,112,256]{2,1,0:T(8,128)(2,1)S(1)}, u32[]{:S(2)}, u32[]{:S(2)}) async-start(bf16[32,112,256]{2,1,0:T(8,128)(2,1)} %branches.1), calls=%async_computation | async-start | bytes 3670016 | tf_op jit(solution)/shard_map/all_to_all | solution.py:356
  93.6 5.5 %copy-start.9 = (bf16[1280,256]{1,0:T(8,128)(2,1)S(1)}, bf16[1280,256]{1,0:T(8,128)(2,1)}, u32[]{:S(2)}) copy-start(bf16[1280,256]{1,0:T(8,128)(2,1)} %param.32) | copy-start | bytes 1966084
  93.9 23.6 %collective-permute-start.7 = (bf16[1,66,48]{2,1,0:T(8,128)(2,1)S(1)}, bf16[1,66,48]{2,1,0:T(8,128)(2,1)S(1)}, u32[]{:S(2)}, u32[]{:S(2)}) collective-permute-start(bf16[1,66,48]{2,1,0:T(8,128)(2,1)S(1)} %get-tuple-element.20), channel_id=1, source_target_pairs={{0,8},{8,16},{16,24},{24,32},{32,40},{40,48},{48,56},{56,64},{64,7... | collective-permute-start | bytes 19016 | tf_op jit(solution)/shard_map/ppermute | solution.py:357
  102.7 16.0 %collective-permute-start.8 = (bf16[1,66,48]{2,1,0:T(8,128)(2,1)S(1)}, bf16[1,66,48]{2,1,0:T(8,128)(2,1)S(1)}, u32[]{:S(2)}, u32[]{:S(2)}) collective-permute-start(bf16[1,66,48]{2,1,0:T(8,128)(2,1)S(1)} %get-tuple-element.19), channel_id=1, source_target_pairs={{8,0},{16,8},{24,16},{32,24},{40,32},{48,40},{56,48},{64,56},{72,6... | collective-permute-start | bytes 19016 | tf_op jit(solution)/shard_map/ppermute | solution.py:358
  (10 other events, 41.6 us)

commit v5 on v4

--- a/solution.py
+++ b/solution.py
@@ -161,13 +161,13 @@
 
 
 def low_kernel(low_features, w_low, b_low, out):
-    value = dot(low_features[...], w_low[...]) + b_low[...]
+    value = dot_t(low_features[...], w_low[...]) + b_low[...]
     out[...] = jnp.maximum(value, 0.0).astype(BF)
 
 
 def tail_kernel(
     received, heads, w_head, b_branch, b_pool, b_proj, blend, low, ups, lows, b_dec,
-    context, decoded, cells, coarse, fine, w_proj, w_up, w_low, sems,
+    context, decoded, cells, coarse, mixes, w_proj, w_up, w_low, sems,
 ):
     copies = [
         pltpu.make_async_copy(source, target, sems.at[index])
@@ -196,17 +196,23 @@
     coarse[PIECE:128, :] = jnp.zeros((16, 256), BF)
     for line in range(4):
         context[line] = cells[18 * line + 19 : 18 * line + 35, :].astype(BF)
-    for across in range(3):
-        fine[across] = dot(blend[across], coarse[...]).astype(BF).reshape(EXT, 64, 256)
     copies[1].wait()
+    for tap in range(9):
+        mixes[128 * tap : 128 * tap + 128, :] = dot(coarse[...], w_up[tap]).astype(BF)
     copies[2].wait()
+
+    def cells_of(tap, first):
+        down, across = divmod(tap, 3)
+        return blend[across, 64 * (first + down) : 64 * (first + down) + 512, :]
+
     for first in (0, 8):
         mixed = jnp.broadcast_to(b_dec[...], (512, 256))
         for down in range(3):
             mixed += dot(low[first + down : first + down + 8].reshape(512, 144), w_low[down])
-            for across in range(3):
-                up = fine[across, first + down : first + down + 8].reshape(512, 256)
-                mixed += dot(up, w_up[3 * down + across])
+        for tap in (0, 2, 4, 6):
+            pair = jnp.concatenate([cells_of(tap, first), cells_of(tap + 1, first)], axis=1)
+            mixed += dot(pair, mixes[128 * tap : 128 * tap + 256, :])
+        mixed += dot(cells_of(8, first), mixes[1024:1152, :])
         decoded[first : first + 8] = jnp.maximum(mixed, 0.0).astype(BF).reshape(8, 64, 256)
 
 
@@ -308,7 +314,7 @@
         in_specs=[pl.BlockSpec(memory_space=pltpu.VMEM)] * 3,
         out_specs=pl.BlockSpec(memory_space=pltpu.VMEM),
         compiler_params=pltpu.CompilerParams(vmem_limit_bytes=4 << 20),
-    )(low_flat, w_low, b_low[None]).reshape(16, 64, 48)
+    )(low_flat, w_low.T, b_low[None]).reshape(16, 64, 48)
     eight = jnp.where(
         yh == 0,
         jnp.concatenate([features, across_y], axis=0),
@@ -374,7 +380,7 @@
         scratch_shapes=[
             pltpu.VMEM((PIECE, 256), F32),
             pltpu.VMEM((128, 256), BF),
-            pltpu.VMEM((3, EXT, 64, 256), BF),
+            pltpu.VMEM((1152, 256), BF),
             pltpu.VMEM((4, 256, 256), BF),
             pltpu.VMEM((9, 256, 256), BF),
             pltpu.VMEM((3, 144, 256), BF),

time: 125 us -> 123 us (0.984)
  transfers between devices with their start and end apart: 10 -> 10, of which waited for: 4 -> 4; matrix products, arithmetic and copies ran while one was open for 8% -> 7% of each run, Pallas kernels for 0% -> 0%
where the time goes in v5:
time: 123 us; the launch traced here: 122 us
  starting transfers between devices  44.4 us (36%)
  blocking collectives  34.5 us (28%)
  waiting for transfers between devices  17.1 us (14%)
  Pallas kernels  16 us (13%)
  local copies, waits for them, and re-layouts  5.77 us (5%)
  other arithmetic  2.43 us (2%)
  between operations  1.28 us (1%)
    all_gather x1, blocking collectives, on_device(): packed = lax.all_gather(unit, 'z', axis=0, tiled=True)  34.5 us
    ppermute x1, starting transfers between devices, on_device(): traded = lax.ppermute(joint, 'core', swap())  14.1 us
    ppermute x1, waiting for transfers between devices, on_device(): top = lax.ppermute(low_mapped[15:], ROWS, shift_pairs(row_count, 1))  13 us
    pallas_call x1, Pallas kernels, on_device(): pl.pallas_call(conv_kernel, name='branches', out_shape=jax.ShapeDtypeStru...  11.9 us
    ppermute x1, starting transfers between devices, on_device(): across_y = lax.ppermute(features, 'yh', swap())  5.77 us
    all_to_all x1, starting transfers between devices, on_device(): received = lax.all_to_all(pieces, BLOCK, 0, 0, tiled=True)  5.14 us
    ppermute x1, starting transfers between devices, on_device(): top = lax.ppermute(low_mapped[15:], ROWS, shift_pairs(row_count, 1))  5.04 us
    ppermute x1, starting transfers between devices, on_device(): far = lax.ppermute(ends, ('z', 'core'), pairs)  4.56 us
  transfers between devices with their start and end apart: 10, of which 4 were waited for; matrix products, arithmetic and copies ran while one was open for 7% of the time, Pallas kernels for 0%

profile of v5, /device:TPU:1, one launch (start us, length us, event | category | flops | bytes accessed | tf_op | source)
XLA Modules:
  0.0 122.4 jit_solution(11111669630629512452)
XLA Ops:
  0.6 5.8 %collective-permute-start = (bf16[4,128,256]{2,1,0:T(8,128)(2,1)}, bf16[4,128,256]{2,1,0:T(8,128)(2,1)S(1)}, u32[]{:S(2)}, u32[]{:S(2)}) collective-permute-start(bf16[4,128,256]{2,1,0:T(8,128)(2,1)} %param.26), channel_id=1, source_target_pairs={{0,16},{16,0},{1,17},{17,1},{2,18},{18,2},{3,19},{19,3},{4,20},{20... | collective-permute-start | bytes 786440 | tf_op jit(solution)/shard_map/ppermute | solution.py:297
  6.4 1.0 convert_reduce_fusion
  7.5 0.9 reshape.124
  8.4 0.9 fusion.2
  9.3 34.5 %all-gather = bf16[1792,256]{1,0:T(8,128)(2,1)S(1)} all-gather(bf16[112,256]{1,0:T(8,128)(2,1)S(1)} %fusion.2), channel_id=2, replica_groups=mesh['z'=16,'yh'=2,'core'=2,'x'=4,'yl'=2] {'z'}, dimensions={0}, use_global_device_ids=true | all-gather | bytes 974848 | tf_op jit(solution)/shard_map/all_gather | solution.py:307
  43.9 1.3 %collective-permute-start.1 = (bf16[8,128,256]{2,1,0:T(8,128)(2,1)S(1)}, bf16[8,128,256]{2,1,0:T(8,128)(2,1)S(1)}, u32[]{:S(2)}, u32[]{:S(2)}) collective-permute-start(bf16[8,128,256]{2,1,0:T(8,128)(2,1)S(1)} %maximum_select_fusion), channel_id=1, source_target_pairs={{0,32},{32,64},{64,96},{96,128},{128,160},{160,192},{192,224},{224... | collective-permute-start | bytes 1572872 | tf_op jit(solution)/shard_map/ppermute | solution.py:328
  45.3 1.3 %collective-permute-start.2 = (bf16[8,128,256]{2,1,0:T(8,128)(2,1)S(1)}, bf16[8,128,256]{2,1,0:T(8,128)(2,1)S(1)}, u32[]{:S(2)}, u32[]{:S(2)}) collective-permute-start(bf16[8,128,256]{2,1,0:T(8,128)(2,1)S(1)} %maximum_select_fusion), channel_id=1, source_target_pairs={{32,0},{64,32},{96,64},{128,96},{160,128},{192,160},{224,192},{256... | collective-permute-start | bytes 1572872 | tf_op jit(solution)/shard_map/ppermute | solution.py:329
  46.6 4.6 %collective-permute-start.3 = (bf16[3,128,256]{2,1,0:T(8,128)(2,1)S(1)}, bf16[3,128,256]{2,1,0:T(8,128)(2,1)S(1)}, u32[]{:S(2)}, u32[]{:S(2)}) collective-permute-start(bf16[3,128,256]{2,1,0:T(8,128)(2,1)S(1)} %select_select_fusion), channel_id=1, source_target_pairs={{8,72},{40,104},{72,136},{104,168},{136,200},{168,232},{200,264},{... | collective-permute-start | bytes 589832 | tf_op jit(solution)/shard_map/ppermute | solution.py:332
  51.5 1.3 %collective-permute-start.5 = (bf16[16,1,48]{2,1,0:T(2,128)(2,1)S(1)}, bf16[16,1,48]{2,1,0:T(2,128)(2,1)S(1)}, u32[]{:S(2)}, u32[]{:S(2)}) collective-permute-start(bf16[16,1,48]{2,1,0:T(2,128)(2,1)S(1)} %get-tuple-element.22), channel_id=1, source_target_pairs={{1,0},{2,1},{3,2},{4,3},{5,4},{6,5},{7,6},{9,8},{10,9},{11,10},{12... | collective-permute-start | bytes 4616 | tf_op jit(solution)/shard_map/ppermute | solution.py:334
  52.8 4.0 %collective-permute-start.4 = (bf16[16,1,48]{2,1,0:T(2,128)(2,1)S(1)}, bf16[16,1,48]{2,1,0:T(2,128)(2,1)S(1)}, u32[]{:S(2)}, u32[]{:S(2)}) collective-permute-start(bf16[16,1,48]{2,1,0:T(2,128)(2,1)S(1)} %get-tuple-element.21), channel_id=1, source_target_pairs={{0,1},{1,2},{2,3},{3,4},{4,5},{5,6},{6,7},{8,9},{9,10},{10,11},{11... | collective-permute-start | bytes 4616 | tf_op jit(solution)/shard_map/ppermute | solution.py:333
  56.8 0.8 collective-permute-done.4
  58.1 14.1 %collective-permute-start.6 = (bf16[27,128,256]{2,1,0:T(8,128)(2,1)S(1)}, bf16[27,128,256]{2,1,0:T(8,128)(2,1)}, u32[]{:S(2)}, u32[]{:S(2)}) collective-permute-start(bf16[27,128,256]{2,1,0:T(8,128)(2,1)S(1)} %pad_maximum_fusion.mine), channel_id=1, source_target_pairs={{0,8},{8,0},{1,9},{9,1},{2,10},{10,2},{3,11},{11,3},{4,12},{12,4},... | collective-permute-start | bytes 5308424 | tf_op jit(solution)/shard_map/ppermute | solution.py:338
  72.2 3.3 %collective-permute-done.6.theirs = bf16[27,128,256]{2,1,0:T(8,128)(2,1)} collective-permute-done((bf16[27,128,256]{2,1,0:T(8,128)(2,1)S(1)}, bf16[27,128,256]{2,1,0:T(8,128)(2,1)}, u32[]{:S(2)}, u32[]{:S(2)}) %collective-permute-start.6) | collective-permute-done | bytes 1769504 | tf_op jit(solution)/shard_map/ppermute | solution.py:338
  75.6 11.9 %branches.1 = bf16[32,112,256]{2,1,0:T(8,128)(2,1)} custom-call(s32[2]{0:T(128)S(1)} %pad_add_fusion.place, bf16[27,128,256]{2,1,0:T(8,128)(2,1)} %copy-done.7, bf16[27,128,256]{2,1,0:T(8,128)(2,1)} %collective-permute-done.6.theirs, bf16[16,112,256]{2,1,0:T(8,128)(2,1)S(1)} %bitcast.22, bf16[256,256]{1,0:T(8,128)(2,1)S(1)} %copy-done.1, ...), custom_call_target="tpu_custom_call" | custom-call | tf_op jit(solution)/shard_map/branches/pallas_call | solution.py:344
  87.6 5.1 %all-to-all-start = ((bf16[32,112,256]{2,1,0:T(8,128)(2,1)}), bf16[32,112,256]{2,1,0:T(8,128)(2,1)S(1)}, u32[]{:S(2)}, u32[]{:S(2)}) async-start(bf16[32,112,256]{2,1,0:T(8,128)(2,1)} %branches.1), calls=%async_computation | async-start | bytes 3670016 | tf_op jit(solution)/shard_map/all_to_all | solution.py:362
  93.1 5.0 %collective-permute-start.7 = (bf16[1,66,48]{2,1,0:T(8,128)(2,1)S(1)}, bf16[1,66,48]{2,1,0:T(8,128)(2,1)S(1)}, u32[]{:S(2)}, u32[]{:S(2)}) collective-permute-start(bf16[1,66,48]{2,1,0:T(8,128)(2,1)S(1)} %get-tuple-element.20), channel_id=1, source_target_pairs={{0,8},{8,16},{16,24},{24,32},{32,40},{40,48},{48,56},{56,64},{64,7... | collective-permute-start | bytes 19016 | tf_op jit(solution)/shard_map/ppermute | solution.py:363
  98.4 0.9 reshape.127
  99.3 1.3 %copy.33 = bf16[4,16,4,4,256]{4,3,1,0,2:T(4,128)(2,1)S(1)} copy(bf16[4,16,4,4,256]{4,3,2,1,0:T(4,128)(2,1)} %reshape.127) | data formatting | bytes 1048576 | tf_op jit(solution)/shard_map/reshape | solution.py:368
  100.6 0.9 reshape.128.heads
  101.8 1.9 %collective-permute-start.8 = (bf16[1,66,48]{2,1,0:T(8,128)(2,1)S(1)}, bf16[1,66,48]{2,1,0:T(8,128)(2,1)S(1)}, u32[]{:S(2)}, u32[]{:S(2)}) collective-permute-start(bf16[1,66,48]{2,1,0:T(8,128)(2,1)S(1)} %get-tuple-element.19), channel_id=1, source_target_pairs={{8,0},{16,8},{24,16},{32,24},{40,32},{48,40},{56,48},{64,56},{72,6... | collective-permute-start | bytes 19016 | tf_op jit(solution)/shard_map/ppermute | solution.py:364
  103.8 13.0 %collective-permute-done.7 = bf16[1,66,48]{2,1,0:T(8,128)(2,1)S(1)} collective-permute-done((bf16[1,66,48]{2,1,0:T(8,128)(2,1)S(1)}, bf16[1,66,48]{2,1,0:T(8,128)(2,1)S(1)}, u32[]{:S(2)}, u32[]{:S(2)}) %collective-permute-start.7) | collective-permute-done | bytes 6368 | tf_op jit(solution)/shard_map/ppermute | solution.py:363
  116.7 1.0 constant_dynamic-update-slice_fusion.1
  118.0 0.5 pad_maximum_fusion.2.low
  118.5 3.9 %decoder.1 = (bf16[4,16,256]{2,1,0:T(8,128)(2,1)}, bf16[16,64,256]{2,1,0:T(8,128)(2,1)}) custom-call(bf16[32,112,256]{2,1,0:T(8,128)(2,1)S(1)} %all-to-all-done.received, bf16[4,256,256]{2,1,0:T(8,128)(2,1)} %reshape.128.heads, bf16[256,256]{1,0:T(8,128)(2,1)S(1)} %slice.52.w_head, f32[4,256]{1,0:T(4,128)S(1)} %reshape.130.b_branch, ...), custom_call_target="tpu_custom_call" | custom-call | tf_op jit(solution)/shard_map/decoder/pallas_call | solution.py:371
  (82 shorter events, 2.1 us)
Async XLA Ops:
  0.6 43.2 %copy-start.8 = (bf16[4,128,256]{2,1,0:T(8,128)(2,1)S(1)}, bf16[4,128,256]{2,1,0:T(8,128)(2,1)}, u32[]{:S(2)}) copy-start(bf16[4,128,256]{2,1,0:T(8,128)(2,1)} %param.26) | copy-start | bytes 786436
  0.6 43.2 %collective-permute-start = (bf16[4,128,256]{2,1,0:T(8,128)(2,1)}, bf16[4,128,256]{2,1,0:T(8,128)(2,1)S(1)}, u32[]{:S(2)}, u32[]{:S(2)}) collective-permute-start(bf16[4,128,256]{2,1,0:T(8,128)(2,1)} %param.26), channel_id=1, source_target_pairs={{0,16},{16,0},{1,17},{17,1},{2,18},{18,2},{3,19},{19,3},{4,20},{20... | collective-permute-start | bytes 786440 | tf_op jit(solution)/shard_map/ppermute | solution.py:297
  7.5 43.7 %copy-start = (bf16[16,64,256]{2,1,0:T(8,128)(2,1)S(1)}, bf16[16,64,256]{2,1,0:T(8,128)(2,1)}, u32[]{:S(2)}) copy-start(bf16[16,64,256]{2,1,0:T(8,128)(2,1)} %param.27) | copy-start | bytes 1572868
  7.5 43.7 %copy-start.3 = (bf16[256,48]{0,1:T(8,128)(2,1)S(1)}, bf16[256,48]{0,1:T(8,128)(2,1)}, u32[]{:S(2)}) copy-start(bf16[256,48]{0,1:T(8,128)(2,1)} %param.34) | copy-start | bytes 73732
  7.5 43.7 %copy-start.6 = (f32[48]{0:T(128)S(1)}, f32[48]{0:T(128)}, u32[]{:S(2)}) copy-start(f32[48]{0:T(128)} %param.35) | copy-start | bytes 580
  43.9 13.8 %collective-permute-start.1 = (bf16[8,128,256]{2,1,0:T(8,128)(2,1)S(1)}, bf16[8,128,256]{2,1,0:T(8,128)(2,1)S(1)}, u32[]{:S(2)}, u32[]{:S(2)}) collective-permute-start(bf16[8,128,256]{2,1,0:T(8,128)(2,1)S(1)} %maximum_select_fusion), channel_id=1, source_target_pairs={{0,32},{32,64},{64,96},{96,128},{128,160},{160,192},{192,224},{224... | collective-permute-start | bytes 1572872 | tf_op jit(solution)/shard_map/ppermute | solution.py:328
  45.3 12.5 %collective-permute-start.2 = (bf16[8,128,256]{2,1,0:T(8,128)(2,1)S(1)}, bf16[8,128,256]{2,1,0:T(8,128)(2,1)S(1)}, u32[]{:S(2)}, u32[]{:S(2)}) collective-permute-start(bf16[8,128,256]{2,1,0:T(8,128)(2,1)S(1)} %maximum_select_fusion), channel_id=1, source_target_pairs={{32,0},{64,32},{96,64},{128,96},{160,128},{192,160},{224,192},{256... | collective-permute-start | bytes 1572872 | tf_op jit(solution)/shard_map/ppermute | solution.py:329
  46.6 11.2 %collective-permute-start.3 = (bf16[3,128,256]{2,1,0:T(8,128)(2,1)S(1)}, bf16[3,128,256]{2,1,0:T(8,128)(2,1)S(1)}, u32[]{:S(2)}, u32[]{:S(2)}) collective-permute-start(bf16[3,128,256]{2,1,0:T(8,128)(2,1)S(1)} %select_select_fusion), channel_id=1, source_target_pairs={{8,72},{40,104},{72,136},{104,168},{136,200},{168,232},{200,264},{... | collective-permute-start | bytes 589832 | tf_op jit(solution)/shard_map/ppermute | solution.py:332
  51.5 5.3 %collective-permute-start.5 = (bf16[16,1,48]{2,1,0:T(2,128)(2,1)S(1)}, bf16[16,1,48]{2,1,0:T(2,128)(2,1)S(1)}, u32[]{:S(2)}, u32[]{:S(2)}) collective-permute-start(bf16[16,1,48]{2,1,0:T(2,128)(2,1)S(1)} %get-tuple-element.22), channel_id=1, source_target_pairs={{1,0},{2,1},{3,2},{4,3},{5,4},{6,5},{7,6},{9,8},{10,9},{11,10},{12... | collective-permute-start | bytes 4616 | tf_op jit(solution)/shard_map/ppermute | solution.py:334
  52.8 4.8 %collective-permute-start.4 = (bf16[16,1,48]{2,1,0:T(2,128)(2,1)S(1)}, bf16[16,1,48]{2,1,0:T(2,128)(2,1)S(1)}, u32[]{:S(2)}, u32[]{:S(2)}) collective-permute-start(bf16[16,1,48]{2,1,0:T(2,128)(2,1)S(1)} %get-tuple-element.21), channel_id=1, source_target_pairs={{0,1},{1,2},{2,3},{3,4},{4,5},{5,6},{6,7},{8,9},{9,10},{10,11},{11... | collective-permute-start | bytes 4616 | tf_op jit(solution)/shard_map/ppermute | solution.py:333
  57.7 35.4 %copy-start.9 = (bf16[16,66,48]{2,1,0:T(8,128)(2,1)}, bf16[16,66,48]{2,1,0:T(8,128)(2,1)S(1)}, u32[]{:S(2)}) copy-start(bf16[16,66,48]{2,1,0:T(8,128)(2,1)S(1)} %pad_maximum_fusion.3) | copy-start | bytes 304132
  57.7 14.5 %copy-start.11 = (f32[64,128]{1,0:T(8,128)S(1)}, f32[64,128]{1,0:T(8,128)}, u32[]{:S(2)}) copy-start(f32[64,128]{1,0:T(8,128)} %constant.72.clone) | copy-start | bytes 98308
  57.7 14.5 %copy-start.12 = (f32[64,128]{1,0:T(8,128)S(1)}, f32[64,128]{1,0:T(8,128)}, u32[]{:S(2)}) copy-start(f32[64,128]{1,0:T(8,128)} %constant.70.clone) | copy-start | bytes 98308
  57.7 14.5 %copy-start.13 = (f32[64,128]{1,0:T(8,128)S(1)}, f32[64,128]{1,0:T(8,128)}, u32[]{:S(2)}) copy-start(f32[64,128]{1,0:T(8,128)} %constant.71.clone) | copy-start | bytes 98308
  57.7 17.8 %copy-start.1 = (bf16[256,256]{1,0:T(8,128)(2,1)S(1)}, bf16[256,256]{1,0:T(8,128)(2,1)}, u32[]{:S(2)}) copy-start(bf16[256,256]{1,0:T(8,128)(2,1)} %w_one.1) | copy-start | bytes 393220
  57.8 17.8 %copy-start.2 = (bf16[256,256]{1,0:T(8,128)(2,1)S(1)}, bf16[256,256]{1,0:T(8,128)(2,1)}, u32[]{:S(2)}) copy-start(bf16[256,256]{1,0:T(8,128)(2,1)} %w_pool.1) | copy-start | bytes 393220
  58.1 17.5 %copy-start.7 = (bf16[27,128,256]{2,1,0:T(8,128)(2,1)}, bf16[27,128,256]{2,1,0:T(8,128)(2,1)S(1)}, u32[]{:S(2)}) copy-start(bf16[27,128,256]{2,1,0:T(8,128)(2,1)S(1)} %pad_maximum_fusion.mine) | copy-start | bytes 5308420
  58.1 17.5 %collective-permute-start.6 = (bf16[27,128,256]{2,1,0:T(8,128)(2,1)S(1)}, bf16[27,128,256]{2,1,0:T(8,128)(2,1)}, u32[]{:S(2)}, u32[]{:S(2)}) collective-permute-start(bf16[27,128,256]{2,1,0:T(8,128)(2,1)S(1)} %pad_maximum_fusion.mine), channel_id=1, source_target_pairs={{0,8},{8,0},{1,9},{9,1},{2,10},{10,2},{3,11},{11,3},{4,12},{12,4},... | collective-permute-start | bytes 5308424 | tf_op jit(solution)/shard_map/ppermute | solution.py:338
  87.5 5.3 %copy-start.14 = (f32[64,128]{1,0:T(8,128)S(1)}, f32[64,128]{1,0:T(8,128)}, u32[]{:S(2)}) copy-start(f32[64,128]{1,0:T(8,128)} %constant.78.clone) | copy-start | bytes 98308
  87.5 5.3 %copy-start.15 = (f32[64,128]{1,0:T(8,128)S(1)}, f32[64,128]{1,0:T(8,128)}, u32[]{:S(2)}) copy-start(f32[64,128]{1,0:T(8,128)} %constant.76.clone) | copy-start | bytes 98308
  87.6 31.0 %all-to-all-start = ((bf16[32,112,256]{2,1,0:T(8,128)(2,1)}), bf16[32,112,256]{2,1,0:T(8,128)(2,1)S(1)}, u32[]{:S(2)}, u32[]{:S(2)}) async-start(bf16[32,112,256]{2,1,0:T(8,128)(2,1)} %branches.1), calls=%async_computation | async-start | bytes 3670016 | tf_op jit(solution)/shard_map/all_to_all | solution.py:362
  92.7 5.5 %copy-start.10 = (bf16[1280,256]{1,0:T(8,128)(2,1)S(1)}, bf16[1280,256]{1,0:T(8,128)(2,1)}, u32[]{:S(2)}) copy-start(bf16[1280,256]{1,0:T(8,128)(2,1)} %param.32) | copy-start | bytes 1966084
  93.1 23.6 %collective-permute-start.7 = (bf16[1,66,48]{2,1,0:T(8,128)(2,1)S(1)}, bf16[1,66,48]{2,1,0:T(8,128)(2,1)S(1)}, u32[]{:S(2)}, u32[]{:S(2)}) collective-permute-start(bf16[1,66,48]{2,1,0:T(8,128)(2,1)S(1)} %get-tuple-element.20), channel_id=1, source_target_pairs={{0,8},{8,16},{16,24},{24,32},{32,40},{40,48},{48,56},{56,64},{64,7... | collective-permute-start | bytes 19016 | tf_op jit(solution)/shard_map/ppermute | solution.py:363
  101.8 16.0 %collective-permute-start.8 = (bf16[1,66,48]{2,1,0:T(8,128)(2,1)S(1)}, bf16[1,66,48]{2,1,0:T(8,128)(2,1)S(1)}, u32[]{:S(2)}, u32[]{:S(2)}) collective-permute-start(bf16[1,66,48]{2,1,0:T(8,128)(2,1)S(1)} %get-tuple-element.19), channel_id=1, source_target_pairs={{8,0},{16,8},{24,16},{32,24},{40,32},{48,40},{56,48},{64,56},{72,6... | collective-permute-start | bytes 19016 | tf_op jit(solution)/shard_map/ppermute | solution.py:364
  (11 other events, 46.9 us)
